TPU v7x, 256 devices: a whole 4x4x8 slice. The times are simulated.
256 devices in a mesh: row: 16 (over z, core), col: 16 (over x, y).
Axes of the slice: x: 4, y: 4, z: 8, core: 2. Of those that a mesh axis runs over, the one named last changes fastest.
Arguments:
- gram: float32 [16, 16, 1024, 1024], P('row', 'col'), may hold values from -21834.348 to 21835.348, as said below
Outputs:
- factored: float32 [16, 16, 1024, 1024], P('row', 'col')
Inputs may be any that keep to these rules, and one draw needn't show every extreme that they name: gram holds a symmetric positive definite matrix of order 16384 whose smallest eigenvalue is at least 1.
All inputs are finite; a program needn't handle non-finite values.
Results may differ from a plain program's by a relative error of at most 0.0001.
Values sent between devices are 32-bit elements; how exact they have to be, the bound alone decides.
No kernel may reach another device: no remote copies, remote signals or barrier semaphores. Data moves between devices by JAX's collectives and lax.ppermute only.
A program may use at most 64 MiB of HBM per device.

v0:
```python
import jax
import jax.numpy as jnp
from jax import lax
from jax.experimental import pallas as pl
from jax.experimental.pallas import tpu as pltpu
from jax.sharding import Mesh
from jax.sharding import PartitionSpec as P

BS = 256
PANELS = 3
WIDTH = PANELS * BS
FACTOR = 128
ROW = ("row_0", "row_1")
COL = ("col_0", "col_1")
FULL = lax.Precision.HIGHEST
UPPER = ((0, 0), (0, 1), (0, 2), (1, 1), (1, 2), (2, 2))


def full_dot(left, right, dims):
    return lax.dot_general(
        left, right, (dims, ((), ())), precision=FULL, preferred_element_type=jnp.float32
    )


def wide(line):
    return jnp.broadcast_to(line, (8, FACTOR))


def factor_inverse(block):
    count = FACTOR // 8
    tiles = [block[8 * b : 8 * b + 8] for b in range(count)]
    lane = lax.broadcasted_iota(jnp.int32, (8, FACTOR), 1)
    sub = lax.broadcasted_iota(jnp.int32, (8, FACTOR), 0)
    for b in range(count):
        cols = {t: [wide(tiles[t][:, 8 * b + j : 8 * b + j + 1]) for j in range(8)] for t in range(b, count)}
        for s in range(8):
            at = lane == 8 * b + s
            own = cols[b]
            inv = 1.0 / wide(own[s][s : s + 1])
            heads = [wide(own[j][s : s + 1]) for j in range(8)]
            pivot = jnp.where(at, 1.0, wide(tiles[b][s : s + 1]))
            for t in range(b, count):
                scale = cols[t][s] * inv
                rest = jnp.where(at, 0.0, tiles[t])
                if t == b:
                    scale = jnp.where(sub > s, scale, 0.0)
                    rest = jnp.where(sub > s, rest, tiles[t])
                for j in range(s + 1, 8):
                    cols[t][j] = cols[t][j] - scale * heads[j]
                tiles[t] = rest - scale * pivot
    rows = []
    for b, tile in enumerate(tiles):
        own = lane == sub + 8 * b
        pivots = jnp.sum(jnp.where(own, tile, 0.0), axis=1, keepdims=True)
        scale = lax.rsqrt(pivots)
        scale = scale * (1.5 - 0.5 * pivots * scale * scale)
        rows.append(jnp.where(lane < sub + 8 * b, tile * scale, jnp.where(own, scale, 0.0)))
    return jnp.concatenate(rows, axis=0)


def corner_kernel(place, mine, other, inverse, work):
    work[...] = jnp.zeros((WIDTH, WIDTH), jnp.float32)
    first = place[0] % 2 == 0
    for n, (i, j) in enumerate(UPPER):
        a, b = mine[:, n % 3].reshape(BS, BS), other[:, n % 3].reshape(BS, BS)
        block = jnp.where(first, a, b) if n < 3 else jnp.where(first, b, a)
        work[i * BS : i * BS + BS, j * BS : j * BS + BS] = block
    for low in range(0, WIDTH, FACTOR):
        high = low + FACTOR
        own = factor_inverse(work[low:high, low:high])
        rows = full_dot(own, work[low:high, :], ((1,), (0,)))
        left = jnp.concatenate([rows[:, :low], own], axis=1) if low else own
        if high == WIDTH:
            inverse[low:high, :] = left
            break
        right = rows[:, high:]
        inverse[low:high, :] = jnp.concatenate([left, jnp.zeros_like(right)], axis=1)
        change = full_dot(right, jnp.concatenate([left, right], axis=1), ((0,), (0,)))
        if low:
            work[high:, :low] = work[high:, :low] - change[:, :low]
        work[high:, low:high] = -change[:, low:high]
        work[high:, high:] = work[high:, high:] - change[:, high:]


IN_VMEM = pl.BlockSpec(memory_space=pltpu.VMEM)
IN_SMEM = pl.BlockSpec(memory_space=pltpu.SMEM)


def corner_inverse(place, mine, other):
    return pl.pallas_call(
        corner_kernel,
        in_specs=[IN_SMEM, IN_VMEM, IN_VMEM],
        out_specs=IN_VMEM,
        out_shape=jax.ShapeDtypeStruct((WIDTH, WIDTH), jnp.float32),
        scratch_shapes=[pltpu.VMEM((WIDTH, WIDTH), jnp.float32)],
        compiler_params=pltpu.CompilerParams(vmem_limit_bytes=56 << 20),
        name="corner",
    )(place, mine, other)


def right_kernel(lines, inverse, out):
    for k in range(PANELS):
        total = None
        for j in range(k + 1):
            part = full_dot(
                inverse[k * BS : k * BS + BS, j * BS : j * BS + BS],
                lines[j * BS : j * BS + BS, :],
                ((1,), (0,)),
            )
            total = part if total is None else total + part
        out[k * BS : k * BS + BS, :] = total


def right_panel(lines, inverse):
    size = lines.shape[1]
    half = size // 2
    return pl.pallas_call(
        right_kernel,
        grid=(2,),
        in_specs=[
            pl.BlockSpec((WIDTH, half), lambda i: (0, i)),
            pl.BlockSpec((WIDTH, WIDTH), lambda i: (0, 0)),
        ],
        out_specs=pl.BlockSpec((WIDTH, half), lambda i: (0, i)),
        out_shape=jax.ShapeDtypeStruct((WIDTH, size), jnp.float32),
        compiler_params=pltpu.CompilerParams(vmem_limit_bytes=56 << 20),
        name="right",
    )(lines, inverse)


def panel_kernel(place, rows, right, inverse, matrix, out, left):
    block_row = pl.program_id(0) * 16 + place[0]
    lines = [rows[:, k, 0].reshape(BS, BS) for k in range(PANELS)]
    for k in range(PANELS):
        total = None
        for j in range(k + 1):
            part = full_dot(lines[j], inverse[k * BS : k * BS + BS, j * BS : j * BS + BS], ((1,), (1,)))
            total = part if total is None else total + part
        left[:, k * BS : k * BS + BS] = total
    out[...] = matrix[...] - full_dot(left[...], right[...], ((1,), (0,)))

    @pl.when(block_row < PANELS)
    def _():
        out[...] = jnp.zeros(out.shape, jnp.float32)

    for k in range(PANELS):

        @pl.when(place[1] == k)
        def _(k=k):
            panel = left[:, k * BS : k * BS + BS]
            r = lax.broadcasted_iota(jnp.int32, (BS, BS), 0) + block_row * BS
            s = lax.broadcasted_iota(jnp.int32, (BS, BS), 1) + k * BS
            out[:, :BS] = jnp.where(r >= s, panel, 0.0)


def panel_update(place, rows, right, inverse, matrix):
    size = matrix.shape[0]
    steps = size // BS
    return pl.pallas_call(
        panel_kernel,
        grid_spec=pltpu.PrefetchScalarGridSpec(
            num_scalar_prefetch=1,
            grid=(steps,),
            in_specs=[
                pl.BlockSpec((16, PANELS, 1, 16, BS), lambda i, _: (0, 0, i, 0, 0)),
                pl.BlockSpec(right.shape, lambda i, _: (0, 0)),
                pl.BlockSpec(inverse.shape, lambda i, _: (0, 0)),
                pl.BlockSpec((BS, size), lambda i, _: (i, 0)),
            ],
            out_specs=pl.BlockSpec((BS, size), lambda i, _: (i, 0)),
            scratch_shapes=[pltpu.VMEM((BS, WIDTH), jnp.float32)],
        ),
        out_shape=jax.ShapeDtypeStruct(matrix.shape, jnp.float32),
        compiler_params=pltpu.CompilerParams(vmem_limit_bytes=56 << 20),
        name="panels",
    )(place, rows, right, inverse, matrix)


def copies(piece):
    return jnp.broadcast_to(piece[None], (16,) + piece.shape)


def exchanged(pieces):
    return lax.all_to_all(pieces, COL, 0, 0, tiled=True)


def swapped(piece):
    return lax.ppermute(piece, "row_1", [(0, 1), (1, 0)])


def corner_pieces(top, z, even):
    last = lax.ppermute(top[2:], ROW, [(2, 1)])
    have = jnp.where(even, top, jnp.concatenate([top[1:], last]))
    near = lax.ppermute(have, "row_0", [(0, 3)])
    far = lax.ppermute(have, "row_0", [(0, 5)])
    have = jnp.where(z == 3, near, jnp.where(z == 5, far, have))
    near = lax.ppermute(have, "row_0", [(0, 1), (3, 2), (5, 6)])
    far = lax.ppermute(have, "row_0", [(0, 7), (3, 4)])
    have = jnp.where((z == 1) | (z == 2) | (z == 6), near, have)
    return jnp.where((z == 7) | (z == 4), far, have)


def on_device(gram):
    matrix = gram[0, 0]
    place = jnp.stack([lax.axis_index(ROW), lax.axis_index(COL)]).astype(jnp.int32)
    lines = lax.all_gather(matrix[:BS], ROW, axis=0, tiled=True)
    slab = matrix[:, :BS].reshape(-1, 16, 16, BS).transpose(1, 0, 2, 3)
    side = exchanged(slab)[:PANELS]
    piece = corner_pieces(side[:, 0], lax.axis_index("row_0"), lax.axis_index("row_1") == 0)
    mine = exchanged(copies(piece))
    other = swapped(mine)
    sides, mine, other = lax.optimization_barrier((copies(side), mine, other))
    rows = exchanged(sides)
    inverse = corner_inverse(place, mine, other)
    return panel_update(place, rows, right_panel(lines, inverse), inverse, matrix)[None, None]


def solution(mesh):
    split = Mesh(mesh.devices.reshape(8, 2, 4, 4), ROW + COL)
    return jax.shard_map(
        on_device,
        mesh=split,
        in_specs=(P(ROW, COL, None, None),),
        out_specs=P(ROW, COL, None, None),
        check_vma=False,
    )
```

profile of v0, /device:TPU:84, one launch (start us, length us, event | category | flops | bytes accessed | tf_op | source)
XLA Modules:
  0.0 155.7 jit_solution(7435556283856662630)
XLA Ops:
  6.5 2.3 %slice.37 = f32[1,1,256,1024]{3,2,1,0:T(8,128)} slice(f32[1,1,1024,1024]{3,2,1,0:T(8,128)} %param.1), slice={[0:1], [0:1], [0:256], [0:1024]} | slice | bytes 2097152 | tf_op jit(solution)/shard_map/slice | solution.py:206
  8.9 0.0 all-gather.3.cloned.1.call-update
  8.9 1.3 slice.39
  10.2 1.1 copy.7
  11.2 7.2 %all-to-all-start = ((f32[16,4,16,256]{3,2,1,0:T(8,128)}), f32[16,4,16,256]{3,2,1,0:T(8,128)S(1)}, u32[]{:S(2)}, u32[]{:S(2)}) async-start(f32[16,4,16,256]{3,2,1,0:T(8,128)} %bitcast.18), calls=%async_computation | async-start | bytes 2097152 | tf_op jit(solution)/shard_map/all_to_all | solution.py:184
  18.5 13.7 %all-to-all-done = f32[16,4,16,256]{3,2,1,0:T(8,128)S(1)} async-done(((f32[16,4,16,256]{3,2,1,0:T(8,128)}), f32[16,4,16,256]{3,2,1,0:T(8,128)S(1)}, u32[]{:S(2)}, u32[]{:S(2)}) %all-to-all-start) | async-done | bytes 1048608 | tf_op jit(solution)/shard_map/all_to_all | solution.py:184
  32.2 0.7 collective-permute-start
  32.9 0.7 collective-permute-start.2
  33.6 0.7 collective-permute-start.1
  34.3 1.3 collective-permute-start.4
  35.6 0.7 collective-permute-start.3
  36.3 15.4 %collective-permute-done.4 = f32[3,16,256]{2,1,0:T(8,128)S(1)} collective-permute-done((f32[3,16,256]{2,1,0:T(8,128)S(1)}, f32[3,16,256]{2,1,0:T(8,128)S(1)}, u32[]{:S(2)}, u32[]{:S(2)}) %collective-permute-start.4) | collective-permute-done | bytes 49184 | tf_op jit(solution)/shard_map/ppermute | solution.py:197
  51.8 0.1 broadcast_in_dim.7
  51.8 14.8 %all_to_all.15.mine = f32[16,3,16,256]{3,2,1,0:T(8,128)S(1)} all-to-all(f32[16,3,16,256]{3,2,1,0:T(8,128)S(1)} %broadcast_in_dim.7), channel_id=1, replica_groups=mesh['row_0'=8,'row_1'=2,'col_0'=4,'col_1'=4] {'col_0','col_1'}, dimensions={0} | all-to-all | bytes 1572864 | tf_op jit(solution)/shard_map/all_to_all | solution.py:184
  66.6 0.9 copy-done.1
  67.6 2.4 %collective-permute-done.5.other = f32[16,3,16,256]{3,2,1,0:T(8,128)} collective-permute-done((f32[16,3,16,256]{3,2,1,0:T(8,128)S(1)}, f32[16,3,16,256]{3,2,1,0:T(8,128)}, u32[]{:S(2)}, u32[]{:S(2)}) %collective-permute-start.5) | collective-permute-done | bytes 786464 | tf_op jit(solution)/shard_map/ppermute | solution.py:188
  70.0 2.1 %broadcast_in_dim.6 = f32[16,3,4,16,256]{4,3,2,1,0:T(8,128)} broadcast(f32[3,4,16,256]{3,2,1,0:T(8,128)S(1)} %slice.40), dimensions={1,2,3,4} | broadcast | bytes 3342336 | tf_op jit(solution)/shard_map/broadcast_in_dim | solution.py:180
  72.0 7.3 %all-to-all-start.2 = ((f32[16,3,4,16,256]{4,3,2,1,0:T(8,128)}), f32[16,3,4,16,256]{4,3,2,1,0:T(8,128)S(1)}, u32[]{:S(2)}, u32[]{:S(2)}) async-start(f32[16,3,4,16,256]{4,3,2,1,0:T(8,128)} %broadcast_in_dim.6), calls=%async_computation.2 | async-start | bytes 6291456 | tf_op jit(solution)/shard_map/all_to_all | solution.py:184
  79.3 0.6 pad_add_fusion.place
  79.9 36.0 %corner.1.inverse = f32[768,768]{1,0:T(8,128)} custom-call(s32[2]{0:T(128)} %pad_add_fusion.place, f32[16,3,16,256]{3,2,1,0:T(8,128)} %copy-done.1, f32[16,3,16,256]{3,2,1,0:T(8,128)} %collective-permute-done.5.other), custom_call_target="tpu_custom_call" | custom-call | tf_op jit(solution)/shard_map/corner/pallas_call | solution.py:90
  115.9 8.9 %right.1 = f32[768,1024]{1,0:T(8,128)} custom-call(f32[4096,1024]{1,0:T(8,128)} %bitcast.19, f32[768,768]{1,0:T(8,128)} %corner.1.inverse), custom_call_target="tpu_custom_call" | custom-call | tf_op jit(solution)/shard_map/right/pallas_call | solution.py:117
  124.7 1.2 all-to-all-done.2.rows
  125.9 1.6 %copy-done = f32[16,3,4,16,256]{4,3,2,1,0:T(8,128)} copy-done((f32[16,3,4,16,256]{4,3,2,1,0:T(8,128)}, f32[16,3,4,16,256]{4,3,2,1,0:T(8,128)S(1)}, u32[]{:S(2)}) %copy-start) | copy-done | bytes 3145752
  127.6 21.3 %panels.1 = f32[1024,1024]{1,0:T(8,128)} custom-call(s32[2]{0:T(128)} %pad_add_fusion.place, f32[16,3,4,16,256]{4,3,2,1,0:T(8,128)} %copy-done, f32[768,1024]{1,0:T(8,128)} %right.1, f32[768,768]{1,0:T(8,128)} %corner.1.inverse, f32[1024,1024]{1,0:T(8,128)} %bitcast.21), custom_call_target="tpu_custom_call" | custom-call | tf_op jit(solution)/shard_map/panels/pallas_call | solution.py:159
  (15 shorter events, 0.1 us)
Async XLA Ops:
  6.5 109.4 %all-gather.3.cloned.1.call-start = ((), (), s32[]{:S(2)}) async-start(), calls=%async_computation.3 | async-start | bytes 17825792 | tf_op jit(solution)/shard_map/all_gather | solution.py:206
  11.2 21.0 %all-to-all-start = ((f32[16,4,16,256]{3,2,1,0:T(8,128)}), f32[16,4,16,256]{3,2,1,0:T(8,128)S(1)}, u32[]{:S(2)}, u32[]{:S(2)}) async-start(f32[16,4,16,256]{3,2,1,0:T(8,128)} %bitcast.18), calls=%async_computation | async-start | bytes 2097152 | tf_op jit(solution)/shard_map/all_to_all | solution.py:184
  32.2 0.7 collective-permute-start
  32.9 1.4 collective-permute-start.2
  33.6 0.7 collective-permute-start.1
  34.3 17.4 %collective-permute-start.4 = (f32[3,16,256]{2,1,0:T(8,128)S(1)}, f32[3,16,256]{2,1,0:T(8,128)S(1)}, u32[]{:S(2)}, u32[]{:S(2)}) collective-permute-start(f32[3,16,256]{2,1,0:T(8,128)S(1)} %select_select_fusion.1), channel_id=1, source_target_pairs={{0,32},{96,64},{160,192},{1,33},{97,65},{161,193},{2,34},{98,66},{... | collective-permute-start | bytes 147464 | tf_op jit(solution)/shard_map/ppermute | solution.py:197
  35.6 16.1 %collective-permute-start.3 = (f32[3,16,256]{2,1,0:T(8,128)S(1)}, f32[3,16,256]{2,1,0:T(8,128)S(1)}, u32[]{:S(2)}, u32[]{:S(2)}) collective-permute-start(f32[3,16,256]{2,1,0:T(8,128)S(1)} %select_select_fusion.1), channel_id=1, source_target_pairs={{0,224},{96,128},{1,225},{97,129},{2,226},{98,130},{3,227},{99,131... | collective-permute-start | bytes 147464 | tf_op jit(solution)/shard_map/ppermute | solution.py:198
  66.6 0.9 copy-start.1
  67.5 2.4 %collective-permute-start.5 = (f32[16,3,16,256]{3,2,1,0:T(8,128)S(1)}, f32[16,3,16,256]{3,2,1,0:T(8,128)}, u32[]{:S(2)}, u32[]{:S(2)}) collective-permute-start(f32[16,3,16,256]{3,2,1,0:T(8,128)S(1)} %all_to_all.15.mine), channel_id=1, source_target_pairs={{0,16},{16,0},{1,17},{17,1},{2,18},{18,2},{3,19},{19,3},{4,20},{20... | collective-permute-start | bytes 2359304 | tf_op jit(solution)/shard_map/ppermute | solution.py:188
  72.0 53.9 %all-to-all-start.2 = ((f32[16,3,4,16,256]{4,3,2,1,0:T(8,128)}), f32[16,3,4,16,256]{4,3,2,1,0:T(8,128)S(1)}, u32[]{:S(2)}, u32[]{:S(2)}) async-start(f32[16,3,4,16,256]{4,3,2,1,0:T(8,128)} %broadcast_in_dim.6), calls=%async_computation.2 | async-start | bytes 6291456 | tf_op jit(solution)/shard_map/all_to_all | solution.py:184
  125.9 1.6 %copy-start = (f32[16,3,4,16,256]{4,3,2,1,0:T(8,128)}, f32[16,3,4,16,256]{4,3,2,1,0:T(8,128)S(1)}, u32[]{:S(2)}) copy-start(f32[16,3,4,16,256]{4,3,2,1,0:T(8,128)S(1)} %all-to-all-done.2.rows) | copy-start | bytes 9437188
Sparse Core Ops, SparseCore 0:
  9.2 96.5 all-gather.2
where the time goes:
time: 156 us
  Pallas kernels  66.1 us (42%)
  waiting for transfers between devices  32.8 us (21%)
  starting transfers between devices  18.4 us (12%)
  blocking collectives  14.8 us (9%)
  between operations  13.5 us (9%)
  local copies, waits for them, and re-layouts  9.42 us (6%)
    pallas_call x1, Pallas kernels, corner_inverse(): pl.pallas_call(corner_kernel, in_specs=[IN_SMEM, IN_VMEM, IN_VMEM], out_s...  36 us
    pallas_call x1, Pallas kernels, panel_update(): pl.pallas_call(panel_kernel, grid_spec=pltpu.PrefetchScalarGridSpec(num_s...  21.3 us
    ppermute x1, waiting for transfers between devices, corner_pieces(): near = lax.ppermute(have, 'row_0', [(0, 1), (3, 2), (5, 6)])  15.4 us
    all_to_all x2, waiting for transfers between devices, exchanged(): return lax.all_to_all(pieces, COL, 0, 0, tiled=True)  14.9 us
    all_to_all x1, blocking collectives, exchanged(): return lax.all_to_all(pieces, COL, 0, 0, tiled=True)  14.8 us
    all_to_all x2, starting transfers between devices, exchanged(): return lax.all_to_all(pieces, COL, 0, 0, tiled=True)  14.5 us
    pallas_call x1, Pallas kernels, right_panel(): pl.pallas_call(right_kernel, grid=(2,), in_specs=[pl.BlockSpec((WIDTH, ha...  8.85 us
  transfers between devices with their start and end apart: 9, of which 4 were waited for; matrix products, arithmetic and copies ran while one was open for 3% of the time, Pallas kernels for 29%

commit v1 on v0

--- a/solution.py
+++ b/solution.py
@@ -20,6 +20,18 @@
     return lax.dot_general(
         left, right, (dims, ((), ())), precision=FULL, preferred_element_type=jnp.float32
     )
+
+
+def split(value):
+    high = value.astype(jnp.bfloat16)
+    return high, (value - high.astype(jnp.float32)).astype(jnp.bfloat16)
+
+
+def split_dot(left, right, dims):
+    def one(a, b):
+        return lax.dot_general(a, b, (dims, ((), ())), preferred_element_type=jnp.float32)
+
+    return one(left[0], right[0]) + (one(left[0], right[1]) + one(left[1], right[0]))
 
 
 def wide(line):
@@ -42,11 +54,11 @@
             for t in range(b, count):
                 scale = cols[t][s] * inv
                 rest = jnp.where(at, 0.0, tiles[t])
+                for j in range(s + 1, 8):
+                    cols[t][j] = cols[t][j] - scale * heads[j]
                 if t == b:
                     scale = jnp.where(sub > s, scale, 0.0)
                     rest = jnp.where(sub > s, rest, tiles[t])
-                for j in range(s + 1, 8):
-                    cols[t][j] = cols[t][j] - scale * heads[j]
                 tiles[t] = rest - scale * pivot
     rows = []
     for b, tile in enumerate(tiles):
@@ -65,21 +77,27 @@
         a, b = mine[:, n % 3].reshape(BS, BS), other[:, n % 3].reshape(BS, BS)
         block = jnp.where(first, a, b) if n < 3 else jnp.where(first, b, a)
         work[i * BS : i * BS + BS, j * BS : j * BS + BS] = block
+    own = factor_inverse(work[:FACTOR, :FACTOR])
     for low in range(0, WIDTH, FACTOR):
-        high = low + FACTOR
-        own = factor_inverse(work[low:high, low:high])
-        rows = full_dot(own, work[low:high, :], ((1,), (0,)))
-        left = jnp.concatenate([rows[:, :low], own], axis=1) if low else own
+        high, after = low + FACTOR, low + 2 * FACTOR
+        if high < WIDTH:
+            right = full_dot(own, work[low:high, high:after], ((1,), (0,)))
+            following = factor_inverse(work[high:after, high:after] - full_dot(right, right, ((0,), (0,))))
+        left = own
+        if low:
+            left = jnp.concatenate([full_dot(own, work[low:high, :low], ((1,), (0,))), own], axis=1)
         if high == WIDTH:
             inverse[low:high, :] = left
             break
-        right = rows[:, high:]
+        if after < WIDTH:
+            right = jnp.concatenate([right, full_dot(own, work[low:high, after:], ((1,), (0,)))], axis=1)
         inverse[low:high, :] = jnp.concatenate([left, jnp.zeros_like(right)], axis=1)
         change = full_dot(right, jnp.concatenate([left, right], axis=1), ((0,), (0,)))
         if low:
             work[high:, :low] = work[high:, :low] - change[:, :low]
         work[high:, low:high] = -change[:, low:high]
         work[high:, high:] = work[high:, high:] - change[:, high:]
+        own = following
 
 
 IN_VMEM = pl.BlockSpec(memory_space=pltpu.VMEM)
@@ -98,46 +116,55 @@
     )(place, mine, other)
 
 
-def right_kernel(lines, inverse, out):
+def right_kernel(lines, inverse, out_high, out_low, inverse_high, inverse_low):
+    @pl.when(pl.program_id(0) == 0)
+    def _():
+        inverse_high[...], inverse_low[...] = split(inverse[...])
+
+    raw = [split(lines[j * BS : j * BS + BS, :]) for j in range(PANELS)]
     for k in range(PANELS):
+        at = slice(k * BS, k * BS + BS)
         total = None
         for j in range(k + 1):
-            part = full_dot(
-                inverse[k * BS : k * BS + BS, j * BS : j * BS + BS],
-                lines[j * BS : j * BS + BS, :],
-                ((1,), (0,)),
-            )
+            by = slice(j * BS, j * BS + BS)
+            part = split_dot((inverse_high[at, by], inverse_low[at, by]), raw[j], ((1,), (0,)))
             total = part if total is None else total + part
-        out[k * BS : k * BS + BS, :] = total
+        out_high[at, :], out_low[at, :] = split(total)
 
 
 def right_panel(lines, inverse):
     size = lines.shape[1]
     half = size // 2
+    part = pl.BlockSpec((WIDTH, half), lambda i: (0, i))
+    whole = pl.BlockSpec((WIDTH, WIDTH), lambda i: (0, 0))
+    wide_shape = jax.ShapeDtypeStruct((WIDTH, size), jnp.bfloat16)
+    square = jax.ShapeDtypeStruct((WIDTH, WIDTH), jnp.bfloat16)
     return pl.pallas_call(
         right_kernel,
         grid=(2,),
-        in_specs=[
-            pl.BlockSpec((WIDTH, half), lambda i: (0, i)),
-            pl.BlockSpec((WIDTH, WIDTH), lambda i: (0, 0)),
-        ],
-        out_specs=pl.BlockSpec((WIDTH, half), lambda i: (0, i)),
-        out_shape=jax.ShapeDtypeStruct((WIDTH, size), jnp.float32),
+        in_specs=[part, whole],
+        out_specs=[part, part, whole, whole],
+        out_shape=[wide_shape, wide_shape, square, square],
         compiler_params=pltpu.CompilerParams(vmem_limit_bytes=56 << 20),
         name="right",
     )(lines, inverse)
 
 
-def panel_kernel(place, rows, right, inverse, matrix, out, left):
+def panel_kernel(place, rows, right_high, right_low, inverse_high, inverse_low, matrix, out, left):
     block_row = pl.program_id(0) * 16 + place[0]
-    lines = [rows[:, k, 0].reshape(BS, BS) for k in range(PANELS)]
+    raw = [split(rows[:, k, 0].reshape(BS, BS)) for k in range(PANELS)]
+    change = None
     for k in range(PANELS):
+        at = slice(k * BS, k * BS + BS)
         total = None
         for j in range(k + 1):
-            part = full_dot(lines[j], inverse[k * BS : k * BS + BS, j * BS : j * BS + BS], ((1,), (1,)))
+            by = slice(j * BS, j * BS + BS)
+            part = split_dot(raw[j], (inverse_high[at, by], inverse_low[at, by]), ((1,), (1,)))
             total = part if total is None else total + part
-        left[:, k * BS : k * BS + BS] = total
-    out[...] = matrix[...] - full_dot(left[...], right[...], ((1,), (0,)))
+        left[:, at] = total
+        part = split_dot(split(total), (right_high[at, :], right_low[at, :]), ((1,), (0,)))
+        change = part if change is None else change + part
+    out[...] = matrix[...] - change
 
     @pl.when(block_row < PANELS)
     def _():
@@ -153,9 +180,11 @@
             out[:, :BS] = jnp.where(r >= s, panel, 0.0)
 
 
-def panel_update(place, rows, right, inverse, matrix):
+def panel_update(place, rows, right, matrix):
     size = matrix.shape[0]
     steps = size // BS
+    wide_spec = pl.BlockSpec((WIDTH, size), lambda i, _: (0, 0))
+    square = pl.BlockSpec((WIDTH, WIDTH), lambda i, _: (0, 0))
     return pl.pallas_call(
         panel_kernel,
         grid_spec=pltpu.PrefetchScalarGridSpec(
@@ -163,8 +192,10 @@
             grid=(steps,),
             in_specs=[
                 pl.BlockSpec((16, PANELS, 1, 16, BS), lambda i, _: (0, 0, i, 0, 0)),
-                pl.BlockSpec(right.shape, lambda i, _: (0, 0)),
-                pl.BlockSpec(inverse.shape, lambda i, _: (0, 0)),
+                wide_spec,
+                wide_spec,
+                square,
+                square,
                 pl.BlockSpec((BS, size), lambda i, _: (i, 0)),
             ],
             out_specs=pl.BlockSpec((BS, size), lambda i, _: (i, 0)),
@@ -173,7 +204,7 @@
         out_shape=jax.ShapeDtypeStruct(matrix.shape, jnp.float32),
         compiler_params=pltpu.CompilerParams(vmem_limit_bytes=56 << 20),
         name="panels",
-    )(place, rows, right, inverse, matrix)
+    )(place, rows, *right, matrix)
 
 
 def copies(piece):
@@ -182,6 +213,34 @@
 
 def exchanged(pieces):
     return lax.all_to_all(pieces, COL, 0, 0, tiled=True)
+
+
+def parts_kernel(matrix, slab, top, done):
+    count = matrix.shape[0]
+    moves = [pltpu.make_async_copy(matrix.at[0], top, done.at[count])]
+    for i in range(count):
+        moves.append(pltpu.make_async_copy(matrix.at[i, :, :, pl.ds(0, BS)], slab.at[:, i], done.at[i]))
+    for move in moves:
+        move.start()
+    for move in moves:
+        move.wait()
+
+
+def parts(matrix):
+    size = matrix.shape[0]
+    count = size // BS
+    in_place = pl.BlockSpec(memory_space=pl.ANY)
+    return pl.pallas_call(
+        parts_kernel,
+        in_specs=[in_place],
+        out_specs=[in_place, in_place],
+        out_shape=[
+            jax.ShapeDtypeStruct((16, count, 16, BS), jnp.float32),
+            jax.ShapeDtypeStruct((16, 16, size), jnp.float32),
+        ],
+        scratch_shapes=[pltpu.SemaphoreType.DMA((count + 1,))],
+        name="parts",
+    )(matrix.reshape(count, 16, 16, size))
 
 
 def swapped(piece):
@@ -203,16 +262,16 @@
 def on_device(gram):
     matrix = gram[0, 0]
     place = jnp.stack([lax.axis_index(ROW), lax.axis_index(COL)]).astype(jnp.int32)
-    lines = lax.all_gather(matrix[:BS], ROW, axis=0, tiled=True)
-    slab = matrix[:, :BS].reshape(-1, 16, 16, BS).transpose(1, 0, 2, 3)
+    slab, top = parts(matrix)
+    lines = lax.all_gather(top.reshape(BS, -1), ROW, axis=0, tiled=True)
     side = exchanged(slab)[:PANELS]
     piece = corner_pieces(side[:, 0], lax.axis_index("row_0"), lax.axis_index("row_1") == 0)
+    place, sides, piece = lax.optimization_barrier((place, copies(side), piece))
     mine = exchanged(copies(piece))
-    other = swapped(mine)
-    sides, mine, other = lax.optimization_barrier((copies(side), mine, other))
+    sides, mine = lax.optimization_barrier((sides, mine))
     rows = exchanged(sides)
-    inverse = corner_inverse(place, mine, other)
-    return panel_update(place, rows, right_panel(lines, inverse), inverse, matrix)[None, None]
+    inverse = corner_inverse(place, mine, swapped(mine))
+    return panel_update(place, rows, right_panel(lines, inverse), matrix)[None, None]
 
 
 def solution(mesh):

time: 156 us -> 204 us (1.31)
  Pallas kernels: 66.1 us -> 120 us
  local copies, waits for them, and re-layouts: 9.42 us -> 4.71 us
    pallas_call x1 -> x2, Pallas kernels: 8.85 us -> 71.4 us  [the longest x1 64.7 us: parts(): pl.pallas_call(parts_kernel, in_specs=[in_place], out_specs=[in_place, in...]
    pallas_call x1, Pallas kernels: 36 us -> 31.1 us  [corner_inverse(): pl.pallas_call(corner_kernel, in_specs=[IN_SMEM, IN_VMEM, IN_VMEM], out_s...]
    pallas_call x1, Pallas kernels: 21.3 us -> 17.3 us  [panel_update(): pl.pallas_call(panel_kernel, grid_spec=pltpu.PrefetchScalarGridSpec(num_s...]
    slice x2 -> x0, local copies, waits for them, and re-layouts: 3.62 us -> none  [the longest x1 2.32 us: on_device(): lines = lax.all_gather(matrix[:BS], ROW, axis=0, tiled=True)]
  transfers between devices with their start and end apart: 9 -> 9, of which waited for: 4 -> 3; matrix products, arithmetic and copies ran while one was open for 3% -> 1% of each run, Pallas kernels for 29% -> 19%
where the time goes in v1:
time: 204 us; the launch traced here: 203 us
  Pallas kernels  120 us (59%)
  waiting for transfers between devices  31 us (15%)
  starting transfers between devices  18.4 us (9%)
  blocking collectives  15.2 us (7%)
  between operations  13.5 us (7%)
  local copies, waits for them, and re-layouts  4.71 us (2%)
    pallas_call x1, Pallas kernels, parts(): pl.pallas_call(parts_kernel, in_specs=[in_place], out_specs=[in_place, in...  64.7 us
    pallas_call x1, Pallas kernels, corner_inverse(): pl.pallas_call(corner_kernel, in_specs=[IN_SMEM, IN_VMEM, IN_VMEM], out_s...  31.1 us
    pallas_call x1, Pallas kernels, panel_update(): pl.pallas_call(panel_kernel, grid_spec=pltpu.PrefetchScalarGridSpec(num_s...  17.3 us
    all_to_all x1, blocking collectives, exchanged(): return lax.all_to_all(pieces, COL, 0, 0, tiled=True)  15.2 us
    ppermute x1, waiting for transfers between devices, corner_pieces(): near = lax.ppermute(have, 'row_0', [(0, 1), (3, 2), (5, 6)])  14.8 us
    all_to_all x2, starting transfers between devices, exchanged(): return lax.all_to_all(pieces, COL, 0, 0, tiled=True)  14.5 us
    all_to_all x2, waiting for transfers between devices, exchanged(): return lax.all_to_all(pieces, COL, 0, 0, tiled=True)  13.8 us
    pallas_call x1, Pallas kernels, right_panel(): pl.pallas_call(right_kernel, grid=(2,), in_specs=[part, whole], out_specs...  6.78 us
  transfers between devices with their start and end apart: 9, of which 3 were waited for; matrix products, arithmetic and copies ran while one was open for 1% of the time, Pallas kernels for 19%

profile of v1, /device:TPU:84, one launch (start us, length us, event | category | flops | bytes accessed | tf_op | source)
XLA Modules:
  0.0 203.5 jit_solution(16869101182901912508)
XLA Ops:
  6.5 64.7 %parts.1 = (f32[16,4,16,256]{3,2,1,0:T(8,128)}, f32[16,16,1024]{2,1,0:T(8,128)}) custom-call(f32[4,16,16,1024]{3,2,1,0:T(8,128)} %bitcast.16), custom_call_target="tpu_custom_call" | custom-call | tf_op jit(solution)/shard_map/parts/pallas_call | solution.py:233
  71.2 0.0 all-gather.2.cloned.1.call-update
  71.2 7.2 %all-to-all-start = ((f32[16,4,16,256]{3,2,1,0:T(8,128)}), f32[16,4,16,256]{3,2,1,0:T(8,128)S(1)}, u32[]{:S(2)}, u32[]{:S(2)}) async-start(f32[16,4,16,256]{3,2,1,0:T(8,128)} %get-tuple-element.16), calls=%async_computation | async-start | bytes 2097152 | tf_op jit(solution)/shard_map/all_to_all | solution.py:215
  78.5 13.7 %all-to-all-done = f32[16,4,16,256]{3,2,1,0:T(8,128)S(1)} async-done(((f32[16,4,16,256]{3,2,1,0:T(8,128)}), f32[16,4,16,256]{3,2,1,0:T(8,128)S(1)}, u32[]{:S(2)}, u32[]{:S(2)}) %all-to-all-start) | async-done | bytes 1048608 | tf_op jit(solution)/shard_map/all_to_all | solution.py:215
  92.2 0.7 collective-permute-start
  92.9 0.0 collective-permute-done
  92.9 0.7 collective-permute-start.2
  93.6 0.7 collective-permute-start.1
  94.3 0.0 collective-permute-done.2
  94.3 0.0 collective-permute-done.1
  94.3 1.3 collective-permute-start.4
  95.6 0.7 collective-permute-start.3
  96.3 0.6 pad_add_fusion.place
  97.0 14.8 %collective-permute-done.4 = f32[3,16,256]{2,1,0:T(8,128)S(1)} collective-permute-done((f32[3,16,256]{2,1,0:T(8,128)S(1)}, f32[3,16,256]{2,1,0:T(8,128)S(1)}, u32[]{:S(2)}, u32[]{:S(2)}) %collective-permute-start.4) | collective-permute-done | bytes 49184 | tf_op jit(solution)/shard_map/ppermute | solution.py:256
  111.8 2.1 %broadcast_in_dim.6 = f32[16,3,4,16,256]{4,3,2,1,0:T(8,128)} broadcast(f32[3,4,16,256]{3,2,1,0:T(8,128)S(1)} %slice.27), dimensions={1,2,3,4} | broadcast | bytes 3342336 | tf_op jit(solution)/shard_map/broadcast_in_dim | solution.py:211
  113.8 0.1 broadcast_in_dim.7
  113.9 15.2 %all_to_all.15.mine = f32[16,3,16,256]{3,2,1,0:T(8,128)} all-to-all(f32[16,3,16,256]{3,2,1,0:T(8,128)S(1)} %broadcast_in_dim.7), channel_id=1, replica_groups=mesh['row_0'=8,'row_1'=2,'col_0'=4,'col_1'=4] {'col_0','col_1'}, dimensions={0} | all-to-all | bytes 1572864 | tf_op jit(solution)/shard_map/all_to_all | solution.py:215
  129.1 7.3 %all-to-all-start.2 = ((f32[16,3,4,16,256]{4,3,2,1,0:T(8,128)}), f32[16,3,4,16,256]{4,3,2,1,0:T(8,128)S(1)}, u32[]{:S(2)}, u32[]{:S(2)}) async-start(f32[16,3,4,16,256]{4,3,2,1,0:T(8,128)} %broadcast_in_dim.6), calls=%async_computation.2 | async-start | bytes 6291456 | tf_op jit(solution)/shard_map/all_to_all | solution.py:215
  136.4 2.5 %collective-permute-done.5.other = f32[16,3,16,256]{3,2,1,0:T(8,128)S(1)} collective-permute-done((f32[16,3,16,256]{3,2,1,0:T(8,128)}, f32[16,3,16,256]{3,2,1,0:T(8,128)S(1)}, u32[]{:S(2)}, u32[]{:S(2)}) %collective-permute-start.5) | collective-permute-done | bytes 786464 | tf_op jit(solution)/shard_map/ppermute | solution.py:247
  138.9 0.9 copy-done.1
  139.8 31.1 %corner.1.inverse = f32[768,768]{1,0:T(8,128)} custom-call(s32[2]{0:T(128)} %pad_add_fusion.place, f32[16,3,16,256]{3,2,1,0:T(8,128)} %all_to_all.15.mine, f32[16,3,16,256]{3,2,1,0:T(8,128)} %copy-done.1), custom_call_target="tpu_custom_call" | custom-call | tf_op jit(solution)/shard_map/corner/pallas_call | solution.py:108
  170.9 6.8 %right.1 = (bf16[768,1024]{1,0:T(8,128)(2,1)}, bf16[768,1024]{1,0:T(8,128)(2,1)}, bf16[768,768]{1,0:T(8,128)(2,1)}, bf16[768,768]{1,0:T(8,128)(2,1)}) custom-call(f32[4096,1024]{1,0:T(8,128)} %all-gather.2.cloned.1.call-done.lines, f32[768,768]{1,0:T(8,128)} %corner.1.inverse), custom_call_target="tpu_custom_call" | custom-call | tf_op jit(solution)/shard_map/right/pallas_call | solution.py:142
  177.7 1.7 copy-done
  179.3 17.3 %panels.1 = f32[1024,1024]{1,0:T(8,128)} custom-call(s32[2]{0:T(128)} %pad_add_fusion.place, f32[16,3,4,16,256]{4,3,2,1,0:T(8,128)} %copy-done, bf16[768,1024]{1,0:T(8,128)(2,1)} %get-tuple-element.23.right_high, bf16[768,1024]{1,0:T(8,128)(2,1)} %get-tuple-element.24.right_low, bf16[768,768]{1,0:T(8,128)(2,1)} %get-tuple-element.25.inverse_high, ...), custom_call_target="tpu_custom_call" | custom-call | tf_op jit(solution)/shard_map/panels/pallas_call | solution.py:188
  (13 shorter events, 0.1 us)
Async XLA Ops:
  6.5 164.4 %all-gather.2.cloned.1.call-start = ((), (), s32[]{:S(2)}) async-start(), calls=%async_computation.3 | async-start | bytes 17825792 | tf_op jit(solution)/shard_map/all_gather | solution.py:266
  71.2 21.0 %all-to-all-start = ((f32[16,4,16,256]{3,2,1,0:T(8,128)}), f32[16,4,16,256]{3,2,1,0:T(8,128)S(1)}, u32[]{:S(2)}, u32[]{:S(2)}) async-start(f32[16,4,16,256]{3,2,1,0:T(8,128)} %get-tuple-element.16), calls=%async_computation | async-start | bytes 2097152 | tf_op jit(solution)/shard_map/all_to_all | solution.py:215
  92.2 0.7 collective-permute-start
  92.9 1.4 collective-permute-start.2
  93.6 0.7 collective-permute-start.1
  94.3 17.4 %collective-permute-start.4 = (f32[3,16,256]{2,1,0:T(8,128)S(1)}, f32[3,16,256]{2,1,0:T(8,128)S(1)}, u32[]{:S(2)}, u32[]{:S(2)}) collective-permute-start(f32[3,16,256]{2,1,0:T(8,128)S(1)} %select_select_fusion.1), channel_id=1, source_target_pairs={{0,32},{96,64},{160,192},{1,33},{97,65},{161,193},{2,34},{98,66},{... | collective-permute-start | bytes 147464 | tf_op jit(solution)/shard_map/ppermute | solution.py:256
  95.6 16.1 %collective-permute-start.3 = (f32[3,16,256]{2,1,0:T(8,128)S(1)}, f32[3,16,256]{2,1,0:T(8,128)S(1)}, u32[]{:S(2)}, u32[]{:S(2)}) collective-permute-start(f32[3,16,256]{2,1,0:T(8,128)S(1)} %select_select_fusion.1), channel_id=1, source_target_pairs={{0,224},{96,128},{1,225},{97,129},{2,226},{98,130},{3,227},{99,131... | collective-permute-start | bytes 147464 | tf_op jit(solution)/shard_map/ppermute | solution.py:257
  129.1 48.6 %all-to-all-start.2 = ((f32[16,3,4,16,256]{4,3,2,1,0:T(8,128)}), f32[16,3,4,16,256]{4,3,2,1,0:T(8,128)S(1)}, u32[]{:S(2)}, u32[]{:S(2)}) async-start(f32[16,3,4,16,256]{4,3,2,1,0:T(8,128)} %broadcast_in_dim.6), calls=%async_computation.2 | async-start | bytes 6291456 | tf_op jit(solution)/shard_map/all_to_all | solution.py:215
  136.4 2.5 %collective-permute-start.5 = (f32[16,3,16,256]{3,2,1,0:T(8,128)}, f32[16,3,16,256]{3,2,1,0:T(8,128)S(1)}, u32[]{:S(2)}, u32[]{:S(2)}) collective-permute-start(f32[16,3,16,256]{3,2,1,0:T(8,128)} %all_to_all.15.mine), channel_id=1, source_target_pairs={{0,16},{16,0},{1,17},{17,1},{2,18},{18,2},{3,19},{19,3},{4,20},{20... | collective-permute-start | bytes 2359304 | tf_op jit(solution)/shard_map/ppermute | solution.py:247
  138.9 0.9 copy-start.1
  177.7 1.7 copy-start
Sparse Core Ops, SparseCore 0:
  71.4 96.5 all-gather.1

commit v2 on v0

v2 whole, which is shorter than its diff:
```python
import jax
import jax.numpy as jnp
from jax import lax
from jax.experimental import pallas as pl
from jax.experimental.pallas import tpu as pltpu
from jax.sharding import Mesh
from jax.sharding import PartitionSpec as P

BS = 256
PANELS = 3
WIDTH = PANELS * BS
FACTOR = 128
ROW = ("row_0", "row_1")
COL = ("col_0", "col_1")
FULL = lax.Precision.HIGHEST
UPPER = ((0, 0), (0, 1), (0, 2), (1, 1), (1, 2), (2, 2))


def full_dot(left, right, dims):
    return lax.dot_general(
        left, right, (dims, ((), ())), precision=FULL, preferred_element_type=jnp.float32
    )


def split(value):
    high = value.astype(jnp.bfloat16)
    return high, (value - high.astype(jnp.float32)).astype(jnp.bfloat16)


def split_dot(left, right, dims):
    by_left, by_right = dims[0][0], dims[1][0]
    return lax.dot_general(
        jnp.concatenate([left[0], left[0], left[1]], axis=by_left),
        jnp.concatenate([right[0], right[1], right[0]], axis=by_right),
        (dims, ((), ())),
        preferred_element_type=jnp.float32,
    )


def wide(line):
    return jnp.broadcast_to(line, (8, FACTOR))


def factor_inverse(block):
    count = FACTOR // 8
    tiles = [block[8 * b : 8 * b + 8] for b in range(count)]
    lane = lax.broadcasted_iota(jnp.int32, (8, FACTOR), 1)
    sub = lax.broadcasted_iota(jnp.int32, (8, FACTOR), 0)
    for b in range(count):
        cols = {t: [wide(tiles[t][:, 8 * b + j : 8 * b + j + 1]) for j in range(8)] for t in range(b, count)}
        for s in range(8):
            at = lane == 8 * b + s
            own = cols[b]
            inv = 1.0 / wide(own[s][s : s + 1])
            heads = [wide(own[j][s : s + 1]) for j in range(8)]
            pivot = jnp.where(at, 1.0, wide(tiles[b][s : s + 1]))
            for t in range(b, count):
                scale = cols[t][s] * inv
                rest = jnp.where(at, 0.0, tiles[t])
                for j in range(s + 1, 8):
                    cols[t][j] = cols[t][j] - scale * heads[j]
                if t == b:
                    scale = jnp.where(sub > s, scale, 0.0)
                    rest = jnp.where(sub > s, rest, tiles[t])
                tiles[t] = rest - scale * pivot
    rows = []
    for b, tile in enumerate(tiles):
        own = lane == sub + 8 * b
        pivots = jnp.sum(jnp.where(own, tile, 0.0), axis=1, keepdims=True)
        scale = lax.rsqrt(pivots)
        scale = scale * (1.5 - 0.5 * pivots * scale * scale)
        rows.append(jnp.where(lane < sub + 8 * b, tile * scale, jnp.where(own, scale, 0.0)))
    return jnp.concatenate(rows, axis=0)


def corner_kernel(place, mine, other, inverse_high, inverse_low, work):
    work[...] = jnp.zeros((WIDTH, WIDTH), jnp.float32)
    first = place[0] % 2 == 0
    for n, (i, j) in enumerate(UPPER):
        a, b = mine[:, n % 3].reshape(BS, BS), other[:, n % 3].reshape(BS, BS)
        block = jnp.where(first, a, b) if n < 3 else jnp.where(first, b, a)
        work[i * BS : i * BS + BS, j * BS : j * BS + BS] = block
    own = factor_inverse(work[:FACTOR, :FACTOR])
    for low in range(0, WIDTH, FACTOR):
        high, after = low + FACTOR, low + 2 * FACTOR
        if high < WIDTH:
            right = full_dot(own, work[low:high, high:after], ((1,), (0,)))
            following = factor_inverse(work[high:after, high:after] - full_dot(right, right, ((0,), (0,))))
        left = own
        if low:
            left = jnp.concatenate([full_dot(own, work[low:high, :low], ((1,), (0,))), own], axis=1)
        if high == WIDTH:
            inverse_high[low:high, :], inverse_low[low:high, :] = split(left)
            break
        if after < WIDTH:
            right = jnp.concatenate([right, full_dot(own, work[low:high, after:], ((1,), (0,)))], axis=1)
        lines = jnp.concatenate([left, jnp.zeros_like(right)], axis=1)
        inverse_high[low:high, :], inverse_low[low:high, :] = split(lines)
        change = full_dot(right, jnp.concatenate([left, right], axis=1), ((0,), (0,)))
        if low:
            work[high:, :low] = work[high:, :low] - change[:, :low]
        work[high:, low:high] = -change[:, low:high]
        work[high:, high:] = work[high:, high:] - change[:, high:]
        own = following


IN_VMEM = pl.BlockSpec(memory_space=pltpu.VMEM)
IN_SMEM = pl.BlockSpec(memory_space=pltpu.SMEM)


def corner_inverse(place, mine, other):
    return pl.pallas_call(
        corner_kernel,
        in_specs=[IN_SMEM, IN_VMEM, IN_VMEM],
        out_specs=[IN_VMEM, IN_VMEM],
        out_shape=[jax.ShapeDtypeStruct((WIDTH, WIDTH), jnp.bfloat16)] * 2,
        scratch_shapes=[pltpu.VMEM((WIDTH, WIDTH), jnp.float32)],
        compiler_params=pltpu.CompilerParams(vmem_limit_bytes=56 << 20),
        name="corner",
    )(place, mine, other)


def panel_kernel(
    place, lines, inverse_high, inverse_low, rows, matrix, out,
    raw_high, raw_low, known_high, known_low, right_high, right_low, left, high, low,
):
    step = pl.program_id(0)

    for k in range(PANELS):
        at, end = slice(k * BS, k * BS + BS), k * BS + BS

        @pl.when(step == k)
        def _(at=at, end=end):
            raw_high[at, :], raw_low[at, :] = split(lines[...])
            known_high[at, :], known_low[at, :] = inverse_high[...], inverse_low[...]
            known = inverse_high[:, :end], inverse_low[:, :end]
            total = split_dot(known, (raw_high[:end, :], raw_low[:end, :]), ((1,), (0,)))
            right_high[at, :], right_low[at, :] = split(total)

    block_row = (step - PANELS) * 16 + place[0]

    @pl.when(step >= PANELS)
    def _():
        for k in range(PANELS):
            at = slice(k * BS, k * BS + BS)
            high[:, at], low[:, at] = split(rows[:, k, 0].reshape(BS, BS))
        for k in range(PANELS):
            at, end = slice(k * BS, k * BS + BS), k * BS + BS
            known = known_high[at, :end], known_low[at, :end]
            left[:, at] = split_dot((high[:, :end], low[:, :end]), known, ((1,), (1,)))
        change = split_dot(split(left[...]), (right_high[...], right_low[...]), ((1,), (0,)))
        out[...] = matrix[...] - change

    @pl.when((step >= PANELS) & (block_row < PANELS))
    def _():
        out[...] = jnp.zeros(out.shape, jnp.float32)

    for k in range(PANELS):

        @pl.when((step >= PANELS) & (place[1] == k))
        def _(k=k):
            panel = left[:, k * BS : k * BS + BS]
            r = lax.broadcasted_iota(jnp.int32, (BS, BS), 0) + block_row * BS
            s = lax.broadcasted_iota(jnp.int32, (BS, BS), 1) + k * BS
            out[:, :BS] = jnp.where(r >= s, panel, 0.0)


def panel_update(place, lines, inverse, rows, matrix):
    size = matrix.shape[0]

    def panel(i, _):
        return jnp.minimum(i, PANELS - 1), 0

    def block(i, _):
        return jnp.maximum(i - PANELS, 0), 0

    narrow = pltpu.VMEM((BS, WIDTH), jnp.bfloat16)
    square = pltpu.VMEM((WIDTH, WIDTH), jnp.bfloat16)
    whole = pltpu.VMEM((WIDTH, size), jnp.bfloat16)
    return pl.pallas_call(
        panel_kernel,
        grid_spec=pltpu.PrefetchScalarGridSpec(
            num_scalar_prefetch=1,
            grid=(PANELS + size // BS,),
            in_specs=[
                pl.BlockSpec((BS, size), panel),
                pl.BlockSpec((BS, WIDTH), panel),
                pl.BlockSpec((BS, WIDTH), panel),
                pl.BlockSpec((16, PANELS, 1, 16, BS), lambda i, _: (0, 0, jnp.maximum(i - PANELS, 0), 0, 0)),
                pl.BlockSpec((BS, size), block),
            ],
            out_specs=pl.BlockSpec((BS, size), block),
            scratch_shapes=[
                whole, whole, square, square, whole, whole,
                pltpu.VMEM((BS, WIDTH), jnp.float32), narrow, narrow,
            ],
        ),
        out_shape=jax.ShapeDtypeStruct(matrix.shape, jnp.float32),
        compiler_params=pltpu.CompilerParams(vmem_limit_bytes=56 << 20),
        name="panels",
    )(place, lines, *inverse, rows, matrix)


def copies(piece):
    return jnp.broadcast_to(piece[None], (16,) + piece.shape)


def exchanged(pieces):
    return lax.all_to_all(pieces, COL, 0, 0, tiled=True)


def swapped(piece):
    return lax.ppermute(piece, "row_1", [(0, 1), (1, 0)])


def corner_pieces(top, z, even):
    last = lax.ppermute(top[2:], ROW, [(2, 1)])
    have = jnp.where(even, top, jnp.concatenate([top[1:], last]))
    near = lax.ppermute(have, "row_0", [(0, 3)])
    far = lax.ppermute(have, "row_0", [(0, 5)])
    have = jnp.where(z == 3, near, jnp.where(z == 5, far, have))
    near = lax.ppermute(have, "row_0", [(0, 1), (3, 2), (5, 6)])
    far = lax.ppermute(have, "row_0", [(0, 7), (3, 4)])
    have = jnp.where((z == 1) | (z == 2) | (z == 6), near, have)
    return jnp.where((z == 7) | (z == 4), far, have)


def on_device(gram):
    matrix = gram[0, 0]
    place = jnp.stack([lax.axis_index(ROW), lax.axis_index(COL)]).astype(jnp.int32)
    slab = matrix[:, :BS].reshape(-1, 16, 16, BS).transpose(1, 0, 2, 3)
    slab, top = lax.optimization_barrier((slab, matrix))
    lines = lax.all_gather(top[:BS], ROW, axis=0, tiled=True)
    side = exchanged(slab)[:PANELS]
    piece = corner_pieces(side[:, 0], lax.axis_index("row_0"), lax.axis_index("row_1") == 0)
    place, sides, piece = lax.optimization_barrier((place, copies(side), piece))
    mine = exchanged(copies(piece))
    sides, mine = lax.optimization_barrier((sides, mine))
    rows = exchanged(sides)
    inverse = corner_inverse(place, mine, swapped(mine))
    return panel_update(place, lines, inverse, rows, matrix)[None, None]


def solution(mesh):
    split = Mesh(mesh.devices.reshape(8, 2, 4, 4), ROW + COL)
    return jax.shard_map(
        on_device,
        mesh=split,
        in_specs=(P(ROW, COL, None, None),),
        out_specs=P(ROW, COL, None, None),
        check_vma=False,
    )
```

time: 156 us -> 140 us (0.90)
  Pallas kernels: 66.1 us -> 47.3 us
  waiting for transfers between devices: 32.8 us -> 35.1 us
    pallas_call x1 -> x0, Pallas kernels: 8.85 us -> none  [right_panel(): pl.pallas_call(right_kernel, grid=(2,), in_specs=[pl.BlockSpec((WIDTH, ha...]
    pallas_call x1, Pallas kernels: 21.3 us -> 16.1 us  [panel_update(): pl.pallas_call(panel_kernel, grid_spec=pltpu.PrefetchScalarGridSpec(num_s...]
    pallas_call x1, Pallas kernels: 36 us -> 31.2 us  [corner_inverse(): pl.pallas_call(corner_kernel, in_specs=[IN_SMEM, IN_VMEM, IN_VMEM], out_s...]
    all_to_all x2, waiting for transfers between devices: 14.9 us -> 17.8 us  [exchanged(): return lax.all_to_all(pieces, COL, 0, 0, tiled=True)]
  transfers between devices with their start and end apart: 9 -> 9, of which waited for: 4 -> 4; matrix products, arithmetic and copies ran while one was open for 3% -> 2% of each run, Pallas kernels for 29% -> 22%
where the time goes in v2:
time: 140 us
  Pallas kernels  47.3 us (34%)
  waiting for transfers between devices  35.1 us (25%)
  starting transfers between devices  18.4 us (13%)
  blocking collectives  15.2 us (11%)
  between operations  13.5 us (10%)
  local copies, waits for them, and re-layouts  9.41 us (7%)
    pallas_call x1, Pallas kernels, corner_inverse(): pl.pallas_call(corner_kernel, in_specs=[IN_SMEM, IN_VMEM, IN_VMEM], out_s...  31.2 us
    all_to_all x2, waiting for transfers between devices, exchanged(): return lax.all_to_all(pieces, COL, 0, 0, tiled=True)  17.8 us
    pallas_call x1, Pallas kernels, panel_update(): pl.pallas_call(panel_kernel, grid_spec=pltpu.PrefetchScalarGridSpec(num_s...  16.1 us
    all_to_all x1, blocking collectives, exchanged(): return lax.all_to_all(pieces, COL, 0, 0, tiled=True)  15.2 us
    ppermute x1, waiting for transfers between devices, corner_pieces(): near = lax.ppermute(have, 'row_0', [(0, 1), (3, 2), (5, 6)])  14.8 us
    all_to_all x2, starting transfers between devices, exchanged(): return lax.all_to_all(pieces, COL, 0, 0, tiled=True)  14.5 us
  transfers between devices with their start and end apart: 9, of which 4 were waited for; matrix products, arithmetic and copies ran while one was open for 2% of the time, Pallas kernels for 22%

profile of v2, /device:TPU:84, one launch (start us, length us, event | category | flops | bytes accessed | tf_op | source)
XLA Modules:
  0.0 139.6 jit_solution(17608737648971206112)
XLA Ops:
  6.5 1.3 slice.35
  7.8 1.1 copy.7
  8.9 2.3 %slice.34 = f32[256,1024]{1,0:T(8,128)} slice(f32[1024,1024]{1,0:T(8,128)} %bitcast.19), slice={[0:256], [0:1024]} | slice | bytes 2097152 | tf_op jit(solution)/shard_map/slice | solution.py:233
  11.2 0.0 all-gather.2.cloned.1.call-update
  11.2 7.2 %all-to-all-start = ((f32[16,4,16,256]{3,2,1,0:T(8,128)}), f32[16,4,16,256]{3,2,1,0:T(8,128)S(1)}, u32[]{:S(2)}, u32[]{:S(2)}) async-start(f32[16,4,16,256]{3,2,1,0:T(8,128)} %bitcast.17), calls=%async_computation | async-start | bytes 2097152 | tf_op jit(solution)/shard_map/all_to_all | solution.py:209
  18.5 13.7 %all-to-all-done = f32[16,4,16,256]{3,2,1,0:T(8,128)S(1)} async-done(((f32[16,4,16,256]{3,2,1,0:T(8,128)}), f32[16,4,16,256]{3,2,1,0:T(8,128)S(1)}, u32[]{:S(2)}, u32[]{:S(2)}) %all-to-all-start) | async-done | bytes 1048608 | tf_op jit(solution)/shard_map/all_to_all | solution.py:209
  32.2 0.7 collective-permute-start
  32.9 0.7 collective-permute-start.2
  33.6 0.7 collective-permute-start.1
  34.3 1.3 collective-permute-start.4
  35.6 0.7 collective-permute-start.3
  36.3 0.6 pad_add_fusion.place
  36.9 14.8 %collective-permute-done.4 = f32[3,16,256]{2,1,0:T(8,128)S(1)} collective-permute-done((f32[3,16,256]{2,1,0:T(8,128)S(1)}, f32[3,16,256]{2,1,0:T(8,128)S(1)}, u32[]{:S(2)}, u32[]{:S(2)}) %collective-permute-start.4) | collective-permute-done | bytes 49184 | tf_op jit(solution)/shard_map/ppermute | solution.py:222
  51.8 2.1 %broadcast_in_dim.6 = f32[16,3,4,16,256]{4,3,2,1,0:T(8,128)} broadcast(f32[3,4,16,256]{3,2,1,0:T(8,128)S(1)} %slice.36), dimensions={1,2,3,4} | broadcast | bytes 3342336 | tf_op jit(solution)/shard_map/broadcast_in_dim | solution.py:205
  53.8 0.1 broadcast_in_dim.7
  53.9 15.2 %all_to_all.15.mine = f32[16,3,16,256]{3,2,1,0:T(8,128)} all-to-all(f32[16,3,16,256]{3,2,1,0:T(8,128)S(1)} %broadcast_in_dim.7), channel_id=1, replica_groups=mesh['row_0'=8,'row_1'=2,'col_0'=4,'col_1'=4] {'col_0','col_1'}, dimensions={0} | all-to-all | bytes 1572864 | tf_op jit(solution)/shard_map/all_to_all | solution.py:209
  69.1 7.3 %all-to-all-start.2 = ((f32[16,3,4,16,256]{4,3,2,1,0:T(8,128)}), f32[16,3,4,16,256]{4,3,2,1,0:T(8,128)S(1)}, u32[]{:S(2)}, u32[]{:S(2)}) async-start(f32[16,3,4,16,256]{4,3,2,1,0:T(8,128)} %broadcast_in_dim.6), calls=%async_computation.2 | async-start | bytes 6291456 | tf_op jit(solution)/shard_map/all_to_all | solution.py:209
  76.4 0.0 collective-permute-start.5
  76.4 2.5 %collective-permute-done.5.other = f32[16,3,16,256]{3,2,1,0:T(8,128)S(1)} collective-permute-done((f32[16,3,16,256]{3,2,1,0:T(8,128)}, f32[16,3,16,256]{3,2,1,0:T(8,128)S(1)}, u32[]{:S(2)}, u32[]{:S(2)}) %collective-permute-start.5) | collective-permute-done | bytes 786464 | tf_op jit(solution)/shard_map/ppermute | solution.py:213
  78.9 0.9 copy-done.1
  79.8 31.2 %corner.1 = (bf16[768,768]{1,0:T(8,128)(2,1)}, bf16[768,768]{1,0:T(8,128)(2,1)}) custom-call(s32[2]{0:T(128)} %pad_add_fusion.place, f32[16,3,16,256]{3,2,1,0:T(8,128)} %all_to_all.15.mine, f32[16,3,16,256]{3,2,1,0:T(8,128)} %copy-done.1), custom_call_target="tpu_custom_call" | custom-call | tf_op jit(solution)/shard_map/corner/pallas_call | solution.py:112
  111.0 4.0 %all-to-all-done.2.rows = f32[16,3,4,16,256]{4,3,2,1,0:T(8,128)S(1)} async-done(((f32[16,3,4,16,256]{4,3,2,1,0:T(8,128)}), f32[16,3,4,16,256]{4,3,2,1,0:T(8,128)S(1)}, u32[]{:S(2)}, u32[]{:S(2)}) %all-to-all-start.2) | async-done | bytes 3145760 | tf_op jit(solution)/shard_map/all_to_all | solution.py:209
  115.0 1.6 %copy-done = f32[16,3,4,16,256]{4,3,2,1,0:T(8,128)} copy-done((f32[16,3,4,16,256]{4,3,2,1,0:T(8,128)}, f32[16,3,4,16,256]{4,3,2,1,0:T(8,128)S(1)}, u32[]{:S(2)}) %copy-start) | copy-done | bytes 3145752
  116.6 16.1 %panels.1 = f32[1024,1024]{1,0:T(8,128)} custom-call(s32[2]{0:T(128)} %pad_add_fusion.place, f32[4096,1024]{1,0:T(8,128)} %all-gather.2.cloned.1.call-done.lines, bf16[768,768]{1,0:T(8,128)(2,1)} %get-tuple-element.20.inverse_high, bf16[768,768]{1,0:T(8,128)(2,1)} %get-tuple-element.21.inverse_low, f32[16,3,4,16,256]{4,3,2,1,0:T(8,128)} %copy-done, ...), custom_call_target="tpu_custom_call" | custom-call | tf_op jit(solution)/shard_map/panels/pallas_call | solution.py:180
  (14 shorter events, 0.1 us)
Async XLA Ops:
  6.5 108.5 %all-gather.2.cloned.1.call-start = ((), (), s32[]{:S(2)}) async-start(), calls=%async_computation.3 | async-start | bytes 17825792 | tf_op jit(solution)/shard_map/all_gather | solution.py:233
  11.2 21.0 %all-to-all-start = ((f32[16,4,16,256]{3,2,1,0:T(8,128)}), f32[16,4,16,256]{3,2,1,0:T(8,128)S(1)}, u32[]{:S(2)}, u32[]{:S(2)}) async-start(f32[16,4,16,256]{3,2,1,0:T(8,128)} %bitcast.17), calls=%async_computation | async-start | bytes 2097152 | tf_op jit(solution)/shard_map/all_to_all | solution.py:209
  32.2 0.7 collective-permute-start
  32.9 1.4 collective-permute-start.2
  33.6 0.7 collective-permute-start.1
  34.3 17.4 %collective-permute-start.4 = (f32[3,16,256]{2,1,0:T(8,128)S(1)}, f32[3,16,256]{2,1,0:T(8,128)S(1)}, u32[]{:S(2)}, u32[]{:S(2)}) collective-permute-start(f32[3,16,256]{2,1,0:T(8,128)S(1)} %select_select_fusion.1), channel_id=1, source_target_pairs={{0,32},{96,64},{160,192},{1,33},{97,65},{161,193},{2,34},{98,66},{... | collective-permute-start | bytes 147464 | tf_op jit(solution)/shard_map/ppermute | solution.py:222
  35.6 16.1 %collective-permute-start.3 = (f32[3,16,256]{2,1,0:T(8,128)S(1)}, f32[3,16,256]{2,1,0:T(8,128)S(1)}, u32[]{:S(2)}, u32[]{:S(2)}) collective-permute-start(f32[3,16,256]{2,1,0:T(8,128)S(1)} %select_select_fusion.1), channel_id=1, source_target_pairs={{0,224},{96,128},{1,225},{97,129},{2,226},{98,130},{3,227},{99,131... | collective-permute-start | bytes 147464 | tf_op jit(solution)/shard_map/ppermute | solution.py:223
  69.1 45.9 %all-to-all-start.2 = ((f32[16,3,4,16,256]{4,3,2,1,0:T(8,128)}), f32[16,3,4,16,256]{4,3,2,1,0:T(8,128)S(1)}, u32[]{:S(2)}, u32[]{:S(2)}) async-start(f32[16,3,4,16,256]{4,3,2,1,0:T(8,128)} %broadcast_in_dim.6), calls=%async_computation.2 | async-start | bytes 6291456 | tf_op jit(solution)/shard_map/all_to_all | solution.py:209
  76.4 2.5 %collective-permute-start.5 = (f32[16,3,16,256]{3,2,1,0:T(8,128)}, f32[16,3,16,256]{3,2,1,0:T(8,128)S(1)}, u32[]{:S(2)}, u32[]{:S(2)}) collective-permute-start(f32[16,3,16,256]{3,2,1,0:T(8,128)} %all_to_all.15.mine), channel_id=1, source_target_pairs={{0,16},{16,0},{1,17},{17,1},{2,18},{18,2},{3,19},{19,3},{4,20},{20... | collective-permute-start | bytes 2359304 | tf_op jit(solution)/shard_map/ppermute | solution.py:213
  78.9 0.9 copy-start.1
  115.0 1.6 %copy-start = (f32[16,3,4,16,256]{4,3,2,1,0:T(8,128)}, f32[16,3,4,16,256]{4,3,2,1,0:T(8,128)S(1)}, u32[]{:S(2)}) copy-start(f32[16,3,4,16,256]{4,3,2,1,0:T(8,128)S(1)} %all-to-all-done.2.rows) | copy-start | bytes 9437188
Sparse Core Ops, SparseCore 0:
  11.4 96.5 all-gather.1

commit v3 on v2

--- a/solution.py
+++ b/solution.py
@@ -27,14 +27,29 @@
     return high, (value - high.astype(jnp.float32)).astype(jnp.bfloat16)
 
 
-def split_dot(left, right, dims):
-    by_left, by_right = dims[0][0], dims[1][0]
-    return lax.dot_general(
-        jnp.concatenate([left[0], left[0], left[1]], axis=by_left),
-        jnp.concatenate([right[0], right[1], right[0]], axis=by_right),
-        (dims, ((), ())),
-        preferred_element_type=jnp.float32,
-    )
+DEEP = 3 * BS
+
+
+def store_hhl(ref, rows, cols, value, axis):
+    high, low = split(value)
+    store_deep(ref, rows, cols, (high, high, low), axis)
+
+
+def store_hlh(ref, rows, cols, value, axis):
+    high, low = split(value)
+    store_deep(ref, rows, cols, (high, low, high), axis)
+
+
+def store_deep(ref, rows, cols, parts, axis):
+    for n, part in enumerate(parts):
+        if axis == 0:
+            ref[rows * DEEP + n * BS : rows * DEEP + n * BS + BS, :] = part
+        else:
+            ref[rows * BS : rows * BS + BS, cols * DEEP + n * BS : cols * DEEP + n * BS + BS] = part
+
+
+def deep_dot(left, right, dims):
+    return lax.dot_general(left, right, (dims, ((), ())), preferred_element_type=jnp.float32)
 
 
 def wide(line):
@@ -74,7 +89,6 @@
 
 
 def corner_kernel(place, mine, other, inverse_high, inverse_low, work):
-    work[...] = jnp.zeros((WIDTH, WIDTH), jnp.float32)
     first = place[0] % 2 == 0
     for n, (i, j) in enumerate(UPPER):
         a, b = mine[:, n % 3].reshape(BS, BS), other[:, n % 3].reshape(BS, BS)
@@ -120,36 +134,33 @@
     )(place, mine, other)
 
 
-def panel_kernel(
-    place, lines, inverse_high, inverse_low, rows, matrix, out,
-    raw_high, raw_low, known_high, known_low, right_high, right_low, left, high, low,
-):
+def panel_kernel(place, lines, inverse_high, inverse_low, rows, matrix, out, raw, known, right, left, side, change):
     step = pl.program_id(0)
 
     for k in range(PANELS):
-        at, end = slice(k * BS, k * BS + BS), k * BS + BS
 
         @pl.when(step == k)
-        def _(at=at, end=end):
-            raw_high[at, :], raw_low[at, :] = split(lines[...])
-            known_high[at, :], known_low[at, :] = inverse_high[...], inverse_low[...]
-            known = inverse_high[:, :end], inverse_low[:, :end]
-            total = split_dot(known, (raw_high[:end, :], raw_low[:end, :]), ((1,), (0,)))
-            right_high[at, :], right_low[at, :] = split(total)
+        def _(k=k):
+            end = DEEP * (k + 1)
+            store_hhl(raw, k, 0, lines[...], 0)
+            for j in range(k + 1):
+                high, low = inverse_high[:, j * BS : j * BS + BS], inverse_low[:, j * BS : j * BS + BS]
+                store_deep(known, k, j, (high, low, high), 1)
+            total = deep_dot(known[k * BS : k * BS + BS, :end], raw[:end, :], ((1,), (0,)))
+            store_hlh(right, k, 0, total, 0)
 
     block_row = (step - PANELS) * 16 + place[0]
 
     @pl.when(step >= PANELS)
     def _():
         for k in range(PANELS):
-            at = slice(k * BS, k * BS + BS)
-            high[:, at], low[:, at] = split(rows[:, k, 0].reshape(BS, BS))
+            store_hhl(side, 0, k, rows[:, k, 0].reshape(BS, BS), 1)
         for k in range(PANELS):
-            at, end = slice(k * BS, k * BS + BS), k * BS + BS
-            known = known_high[at, :end], known_low[at, :end]
-            left[:, at] = split_dot((high[:, :end], low[:, :end]), known, ((1,), (1,)))
-        change = split_dot(split(left[...]), (right_high[...], right_low[...]), ((1,), (0,)))
-        out[...] = matrix[...] - change
+            at, end = slice(k * BS, k * BS + BS), DEEP * (k + 1)
+            total = deep_dot(side[:, :end], known[at, :end], ((1,), (1,)))
+            left[:, at] = total
+            store_hhl(change, 0, k, total, 1)
+        out[...] = matrix[...] - deep_dot(change[...], right[...], ((1,), (0,)))
 
     @pl.when((step >= PANELS) & (block_row < PANELS))
     def _():
@@ -174,9 +185,7 @@
     def block(i, _):
         return jnp.maximum(i - PANELS, 0), 0
 
-    narrow = pltpu.VMEM((BS, WIDTH), jnp.bfloat16)
-    square = pltpu.VMEM((WIDTH, WIDTH), jnp.bfloat16)
-    whole = pltpu.VMEM((WIDTH, size), jnp.bfloat16)
+    deep = 3 * WIDTH
     return pl.pallas_call(
         panel_kernel,
         grid_spec=pltpu.PrefetchScalarGridSpec(
@@ -191,8 +200,12 @@
             ],
             out_specs=pl.BlockSpec((BS, size), block),
             scratch_shapes=[
-                whole, whole, square, square, whole, whole,
-                pltpu.VMEM((BS, WIDTH), jnp.float32), narrow, narrow,
+                pltpu.VMEM((deep, size), jnp.bfloat16),
+                pltpu.VMEM((WIDTH, deep), jnp.bfloat16),
+                pltpu.VMEM((deep, size), jnp.bfloat16),
+                pltpu.VMEM((BS, WIDTH), jnp.float32),
+                pltpu.VMEM((BS, deep), jnp.bfloat16),
+                pltpu.VMEM((BS, deep), jnp.bfloat16),
             ],
         ),
         out_shape=jax.ShapeDtypeStruct(matrix.shape, jnp.float32),
@@ -228,14 +241,13 @@
 def on_device(gram):
     matrix = gram[0, 0]
     place = jnp.stack([lax.axis_index(ROW), lax.axis_index(COL)]).astype(jnp.int32)
-    slab = matrix[:, :BS].reshape(-1, 16, 16, BS).transpose(1, 0, 2, 3)
-    slab, top = lax.optimization_barrier((slab, matrix))
-    lines = lax.all_gather(top[:BS], ROW, axis=0, tiled=True)
+    top, below = lax.optimization_barrier((matrix[:BS], matrix))
+    lines = lax.all_gather(top, ROW, axis=0, tiled=True)
+    slab = below[:, :BS].reshape(-1, 16, 16, BS).transpose(1, 0, 2, 3)
     side = exchanged(slab)[:PANELS]
     piece = corner_pieces(side[:, 0], lax.axis_index("row_0"), lax.axis_index("row_1") == 0)
-    place, sides, piece = lax.optimization_barrier((place, copies(side), piece))
     mine = exchanged(copies(piece))
-    sides, mine = lax.optimization_barrier((sides, mine))
+    place, sides, mine = lax.optimization_barrier((place, copies(side), mine))
     rows = exchanged(sides)
     inverse = corner_inverse(place, mine, swapped(mine))
     return panel_update(place, lines, inverse, rows, matrix)[None, None]

time: 140 us -> 141 us (level)
  blocking collectives: 15.2 us -> 0 us
  starting transfers between devices: 18.4 us -> 26.3 us
  waiting for transfers between devices: 35.1 us -> 42.5 us
    all_to_all x1 -> x0, blocking collectives: 15.2 us -> none  [exchanged(): return lax.all_to_all(pieces, COL, 0, 0, tiled=True)]
    all_to_all x2 -> x3, starting transfers between devices: 14.5 us -> 22.3 us  [exchanged(): return lax.all_to_all(pieces, COL, 0, 0, tiled=True)]
    all_to_all x2 -> x3, waiting for transfers between devices: 17.8 us -> 24.6 us  [exchanged(): return lax.all_to_all(pieces, COL, 0, 0, tiled=True)]
  transfers between devices with their start and end apart: 9 -> 10, of which waited for: 4 -> 5; matrix products, arithmetic and copies ran while one was open for 2% -> 4% of each run, Pallas kernels for 22% -> 22%
where the time goes in v3:
time: 141 us
  Pallas kernels  47.5 us (34%)
  waiting for transfers between devices  42.5 us (30%)
  starting transfers between devices  26.3 us (19%)
  between operations  13.5 us (10%)
  local copies, waits for them, and re-layouts  10.3 us (7%)
    pallas_call x1, Pallas kernels, corner_inverse(): pl.pallas_call(corner_kernel, in_specs=[IN_SMEM, IN_VMEM, IN_VMEM], out_s...  31.4 us
    all_to_all x3, waiting for transfers between devices, exchanged(): return lax.all_to_all(pieces, COL, 0, 0, tiled=True)  24.6 us
    all_to_all x3, starting transfers between devices, exchanged(): return lax.all_to_all(pieces, COL, 0, 0, tiled=True)  22.3 us
    pallas_call x1, Pallas kernels, panel_update(): pl.pallas_call(panel_kernel, grid_spec=pltpu.PrefetchScalarGridSpec(num_s...  16.1 us
    ppermute x1, waiting for transfers between devices, corner_pieces(): near = lax.ppermute(have, 'row_0', [(0, 1), (3, 2), (5, 6)])  15.4 us
    broadcast_in_dim x2, local copies, waits for them, and re-layouts, copies(): return jnp.broadcast_to(piece[None], (16,) + piece.shape)  3.04 us
  transfers between devices with their start and end apart: 10, of which 5 were waited for; matrix products, arithmetic and copies ran while one was open for 4% of the time, Pallas kernels for 22%

profile of v3, /device:TPU:84, one launch (start us, length us, event | category | flops | bytes accessed | tf_op | source)
XLA Modules:
  0.0 140.8 jit_solution(5563207116448821734)
XLA Ops:
  6.5 2.3 %slice_bitcast_fusion = f32[256,1024]{1,0:T(8,128)} fusion(f32[1,1,1024,1024]{3,2,1,0:T(8,128)} %param.1), kind=kLoop, calls=%fused_computation.1 | loop fusion | bytes 2097152 | tf_op jit(solution)/shard_map/slice | solution.py:244
  8.9 0.0 all-gather.2.cloned.1.call-update
  8.9 1.3 slice.32
  10.2 1.1 copy.7
  11.3 7.2 %all-to-all-start = ((f32[16,4,16,256]{3,2,1,0:T(8,128)}), f32[16,4,16,256]{3,2,1,0:T(8,128)S(1)}, u32[]{:S(2)}, u32[]{:S(2)}) async-start(f32[16,4,16,256]{3,2,1,0:T(8,128)} %bitcast.19), calls=%async_computation | async-start | bytes 2097152 | tf_op jit(solution)/shard_map/all_to_all | solution.py:222
  18.5 13.7 %all-to-all-done = f32[16,4,16,256]{3,2,1,0:T(8,128)S(1)} async-done(((f32[16,4,16,256]{3,2,1,0:T(8,128)}), f32[16,4,16,256]{3,2,1,0:T(8,128)S(1)}, u32[]{:S(2)}, u32[]{:S(2)}) %all-to-all-start) | async-done | bytes 1048608 | tf_op jit(solution)/shard_map/all_to_all | solution.py:222
  32.2 0.7 collective-permute-start
  32.9 0.7 collective-permute-start.2
  33.6 0.7 collective-permute-start.1
  34.3 1.3 collective-permute-start.4
  35.6 0.7 collective-permute-start.3
  36.3 15.4 %collective-permute-done.4 = f32[3,16,256]{2,1,0:T(8,128)S(1)} collective-permute-done((f32[3,16,256]{2,1,0:T(8,128)S(1)}, f32[3,16,256]{2,1,0:T(8,128)S(1)}, u32[]{:S(2)}, u32[]{:S(2)}) %collective-permute-start.4) | collective-permute-done | bytes 49184 | tf_op jit(solution)/shard_map/ppermute | solution.py:235
  51.8 1.0 broadcast_in_dim.7
  52.7 7.7 %all-to-all-start.1 = ((f32[16,3,16,256]{3,2,1,0:T(8,128)}), f32[16,3,16,256]{3,2,1,0:T(8,128)S(1)}, u32[]{:S(2)}, u32[]{:S(2)}) async-start(f32[16,3,16,256]{3,2,1,0:T(8,128)} %broadcast_in_dim.7), calls=%async_computation.1 | async-start | bytes 1572864 | tf_op jit(solution)/shard_map/all_to_all | solution.py:222
  60.5 0.6 pad_add_fusion.place
  61.1 7.2 %all-to-all-done.1.mine = f32[16,3,16,256]{3,2,1,0:T(8,128)S(1)} async-done(((f32[16,3,16,256]{3,2,1,0:T(8,128)}), f32[16,3,16,256]{3,2,1,0:T(8,128)S(1)}, u32[]{:S(2)}, u32[]{:S(2)}) %all-to-all-start.1) | async-done | bytes 786464 | tf_op jit(solution)/shard_map/all_to_all | solution.py:222
  68.3 2.1 %broadcast_in_dim.6 = f32[16,3,4,16,256]{4,3,2,1,0:T(8,128)} broadcast(f32[3,4,16,256]{3,2,1,0:T(8,128)S(1)} %slice.39), dimensions={1,2,3,4} | broadcast | bytes 3342336 | tf_op jit(solution)/shard_map/broadcast_in_dim | solution.py:218
  70.4 7.4 %all-to-all-start.2 = ((f32[16,3,4,16,256]{4,3,2,1,0:T(8,128)}), f32[16,3,4,16,256]{4,3,2,1,0:T(8,128)S(1)}, u32[]{:S(2)}, u32[]{:S(2)}) async-start(f32[16,3,4,16,256]{4,3,2,1,0:T(8,128)} %broadcast_in_dim.6), calls=%async_computation.2 | async-start | bytes 6291456 | tf_op jit(solution)/shard_map/all_to_all | solution.py:222
  77.8 2.5 %collective-permute-done.5.other = f32[16,3,16,256]{3,2,1,0:T(8,128)S(1)} collective-permute-done((f32[16,3,16,256]{3,2,1,0:T(8,128)}, f32[16,3,16,256]{3,2,1,0:T(8,128)S(1)}, u32[]{:S(2)}, u32[]{:S(2)}) %collective-permute-start.5) | collective-permute-done | bytes 786464 | tf_op jit(solution)/shard_map/ppermute | solution.py:226
  80.3 0.9 copy-done.2
  81.2 31.4 %corner.1 = (bf16[768,768]{1,0:T(8,128)(2,1)}, bf16[768,768]{1,0:T(8,128)(2,1)}) custom-call(s32[2]{0:T(128)} %pad_add_fusion.place, f32[16,3,16,256]{3,2,1,0:T(8,128)} %copy-done.1, f32[16,3,16,256]{3,2,1,0:T(8,128)} %copy-done.2), custom_call_target="tpu_custom_call" | custom-call | tf_op jit(solution)/shard_map/corner/pallas_call | solution.py:126
  112.6 3.6 %all-to-all-done.2.rows = f32[16,3,4,16,256]{4,3,2,1,0:T(8,128)S(1)} async-done(((f32[16,3,4,16,256]{4,3,2,1,0:T(8,128)}), f32[16,3,4,16,256]{4,3,2,1,0:T(8,128)S(1)}, u32[]{:S(2)}, u32[]{:S(2)}) %all-to-all-start.2) | async-done | bytes 3145760 | tf_op jit(solution)/shard_map/all_to_all | solution.py:222
  116.2 1.6 %copy-done = f32[16,3,4,16,256]{4,3,2,1,0:T(8,128)} copy-done((f32[16,3,4,16,256]{4,3,2,1,0:T(8,128)}, f32[16,3,4,16,256]{4,3,2,1,0:T(8,128)S(1)}, u32[]{:S(2)}) %copy-start) | copy-done | bytes 3145752
  117.8 16.1 %panels.1 = f32[1024,1024]{1,0:T(8,128)} custom-call(s32[2]{0:T(128)} %pad_add_fusion.place, f32[4096,1024]{1,0:T(8,128)} %all-gather.2.cloned.1.call-done.lines, bf16[768,768]{1,0:T(8,128)(2,1)} %get-tuple-element.16.inverse_high, bf16[768,768]{1,0:T(8,128)(2,1)} %get-tuple-element.17.inverse_low, f32[16,3,4,16,256]{4,3,2,1,0:T(8,128)} %copy-done, ...), custom_call_target="tpu_custom_call" | custom-call | tf_op jit(solution)/shard_map/panels/pallas_call | solution.py:189
  (17 shorter events, 0.1 us)
Async XLA Ops:
  6.5 109.7 %all-gather.2.cloned.1.call-start = ((), (), s32[]{:S(2)}) async-start(), calls=%async_computation.3 | async-start | bytes 17825792 | tf_op jit(solution)/shard_map/all_gather | solution.py:245
  11.3 21.0 %all-to-all-start = ((f32[16,4,16,256]{3,2,1,0:T(8,128)}), f32[16,4,16,256]{3,2,1,0:T(8,128)S(1)}, u32[]{:S(2)}, u32[]{:S(2)}) async-start(f32[16,4,16,256]{3,2,1,0:T(8,128)} %bitcast.19), calls=%async_computation | async-start | bytes 2097152 | tf_op jit(solution)/shard_map/all_to_all | solution.py:222
  32.2 0.7 collective-permute-start
  32.9 1.4 collective-permute-start.2
  33.6 0.7 collective-permute-start.1
  34.3 17.4 %collective-permute-start.4 = (f32[3,16,256]{2,1,0:T(8,128)S(1)}, f32[3,16,256]{2,1,0:T(8,128)S(1)}, u32[]{:S(2)}, u32[]{:S(2)}) collective-permute-start(f32[3,16,256]{2,1,0:T(8,128)S(1)} %select_select_fusion.1), channel_id=1, source_target_pairs={{0,32},{96,64},{160,192},{1,33},{97,65},{161,193},{2,34},{98,66},{... | collective-permute-start | bytes 147464 | tf_op jit(solution)/shard_map/ppermute | solution.py:235
  35.6 16.1 %collective-permute-start.3 = (f32[3,16,256]{2,1,0:T(8,128)S(1)}, f32[3,16,256]{2,1,0:T(8,128)S(1)}, u32[]{:S(2)}, u32[]{:S(2)}) collective-permute-start(f32[3,16,256]{2,1,0:T(8,128)S(1)} %select_select_fusion.1), channel_id=1, source_target_pairs={{0,224},{96,128},{1,225},{97,129},{2,226},{98,130},{3,227},{99,131... | collective-permute-start | bytes 147464 | tf_op jit(solution)/shard_map/ppermute | solution.py:236
  52.7 15.6 %all-to-all-start.1 = ((f32[16,3,16,256]{3,2,1,0:T(8,128)}), f32[16,3,16,256]{3,2,1,0:T(8,128)S(1)}, u32[]{:S(2)}, u32[]{:S(2)}) async-start(f32[16,3,16,256]{3,2,1,0:T(8,128)} %broadcast_in_dim.7), calls=%async_computation.1 | async-start | bytes 1572864 | tf_op jit(solution)/shard_map/all_to_all | solution.py:222
  68.3 2.1 %copy-start.1 = (f32[16,3,16,256]{3,2,1,0:T(8,128)}, f32[16,3,16,256]{3,2,1,0:T(8,128)S(1)}, u32[]{:S(2)}) copy-start(f32[16,3,16,256]{3,2,1,0:T(8,128)S(1)} %all-to-all-done.1.mine) | copy-start | bytes 2359300
  70.4 45.8 %all-to-all-start.2 = ((f32[16,3,4,16,256]{4,3,2,1,0:T(8,128)}), f32[16,3,4,16,256]{4,3,2,1,0:T(8,128)S(1)}, u32[]{:S(2)}, u32[]{:S(2)}) async-start(f32[16,3,4,16,256]{4,3,2,1,0:T(8,128)} %broadcast_in_dim.6), calls=%async_computation.2 | async-start | bytes 6291456 | tf_op jit(solution)/shard_map/all_to_all | solution.py:222
  77.8 2.5 %collective-permute-start.5 = (f32[16,3,16,256]{3,2,1,0:T(8,128)}, f32[16,3,16,256]{3,2,1,0:T(8,128)S(1)}, u32[]{:S(2)}, u32[]{:S(2)}) collective-permute-start(f32[16,3,16,256]{3,2,1,0:T(8,128)} %copy-done.1), channel_id=1, source_target_pairs={{0,16},{16,0},{1,17},{17,1},{2,18},{18,2},{3,19},{19,3},{4,20},{20... | collective-permute-start | bytes 2359304 | tf_op jit(solution)/shard_map/ppermute | solution.py:226
  80.3 0.9 copy-start.2
  116.2 1.6 %copy-start = (f32[16,3,4,16,256]{4,3,2,1,0:T(8,128)}, f32[16,3,4,16,256]{4,3,2,1,0:T(8,128)S(1)}, u32[]{:S(2)}) copy-start(f32[16,3,4,16,256]{4,3,2,1,0:T(8,128)S(1)} %all-to-all-done.2.rows) | copy-start | bytes 9437188
Sparse Core Ops, SparseCore 0:
  9.2 96.5 all-gather.1

commit v4 on v2

--- a/solution.py
+++ b/solution.py
@@ -214,11 +214,13 @@
 
 
 def corner_pieces(top, z, even):
-    last = lax.ppermute(top[2:], ROW, [(2, 1)])
-    have = jnp.where(even, top, jnp.concatenate([top[1:], last]))
+    have = jnp.where(even, top, jnp.concatenate([top[1:], top[2:]]))
     near = lax.ppermute(have, "row_0", [(0, 3)])
     far = lax.ppermute(have, "row_0", [(0, 5)])
+    last = [lax.ppermute(top[2:], ROW, [(2, 2 * at + 1)]) for at in (0, 3, 5)]
     have = jnp.where(z == 3, near, jnp.where(z == 5, far, have))
+    last = jnp.where(z == 3, last[1], jnp.where(z == 5, last[2], last[0]))
+    have = jnp.concatenate([have[:2], jnp.where(even, have[2:], last)])
     near = lax.ppermute(have, "row_0", [(0, 1), (3, 2), (5, 6)])
     far = lax.ppermute(have, "row_0", [(0, 7), (3, 4)])
     have = jnp.where((z == 1) | (z == 2) | (z == 6), near, have)
@@ -228,16 +230,17 @@
 def on_device(gram):
     matrix = gram[0, 0]
     place = jnp.stack([lax.axis_index(ROW), lax.axis_index(COL)]).astype(jnp.int32)
-    slab = matrix[:, :BS].reshape(-1, 16, 16, BS).transpose(1, 0, 2, 3)
-    slab, top = lax.optimization_barrier((slab, matrix))
-    lines = lax.all_gather(top[:BS], ROW, axis=0, tiled=True)
+    top, below = lax.optimization_barrier((matrix[:BS], matrix))
+    lines = lax.all_gather(top, ROW, axis=0, tiled=True)
+    slab = below[:, :BS].reshape(-1, 16, 16, BS).transpose(1, 0, 2, 3)
     side = exchanged(slab)[:PANELS]
     piece = corner_pieces(side[:, 0], lax.axis_index("row_0"), lax.axis_index("row_1") == 0)
     place, sides, piece = lax.optimization_barrier((place, copies(side), piece))
     mine = exchanged(copies(piece))
-    sides, mine = lax.optimization_barrier((sides, mine))
+    other = swapped(mine)
+    sides, mine, other = lax.optimization_barrier((sides, mine, other))
     rows = exchanged(sides)
-    inverse = corner_inverse(place, mine, swapped(mine))
+    inverse = corner_inverse(place, mine, other)
     return panel_update(place, lines, inverse, rows, matrix)[None, None]
 
 

time: 140 us -> 154 us (1.10)
  the two profiles are of different devices: /device:TPU:84 before, /device:TPU:124 now
where the time goes in v4:
time: 154 us; the launch traced here: 153 us
  Pallas kernels  47.4 us (31%)
  waiting for transfers between devices  42 us (27%)
  starting transfers between devices  21.3 us (14%)
  blocking collectives  19 us (12%)
  between operations  13.6 us (9%)
  local copies, waits for them, and re-layouts  9.4 us (6%)
    pallas_call x1, Pallas kernels, corner_inverse(): pl.pallas_call(corner_kernel, in_specs=[IN_SMEM, IN_VMEM, IN_VMEM], out_s...  31.2 us
    all_to_all x2, waiting for transfers between devices, exchanged(): return lax.all_to_all(pieces, COL, 0, 0, tiled=True)  29.3 us
    all_to_all x1, blocking collectives, exchanged(): return lax.all_to_all(pieces, COL, 0, 0, tiled=True)  19 us
    pallas_call x1, Pallas kernels, panel_update(): pl.pallas_call(panel_kernel, grid_spec=pltpu.PrefetchScalarGridSpec(num_s...  16.1 us
    all_to_all x2, starting transfers between devices, exchanged(): return lax.all_to_all(pieces, COL, 0, 0, tiled=True)  14.5 us
    ppermute x1, waiting for transfers between devices, corner_pieces(): near = lax.ppermute(have, 'row_0', [(0, 3)])  8.22 us
  transfers between devices with their start and end apart: 11, of which 6 were waited for; matrix products, arithmetic and copies ran while one was open for 3% of the time, Pallas kernels for 20%

profile of v4, /device:TPU:124, one launch (start us, length us, event | category | flops | bytes accessed | tf_op | source)
XLA Modules:
  0.0 153.3 jit_solution(10252034604151754621)
XLA Ops:
  6.5 2.3 %slice_bitcast_fusion = f32[256,1024]{1,0:T(8,128)} fusion(f32[1,1,1024,1024]{3,2,1,0:T(8,128)} %param.1), kind=kLoop, calls=%fused_computation.1 | loop fusion | bytes 2097152 | tf_op jit(solution)/shard_map/slice | solution.py:233
  8.9 1.3 slice.41
  10.2 1.1 copy.9
  11.3 7.1 %all-to-all-start = ((f32[16,4,16,256]{3,2,1,0:T(8,128)}), f32[16,4,16,256]{3,2,1,0:T(8,128)S(1)}, u32[]{:S(2)}, u32[]{:S(2)}) async-start(f32[16,4,16,256]{3,2,1,0:T(8,128)} %bitcast.21), calls=%async_computation | async-start | bytes 2097152 | tf_op jit(solution)/shard_map/all_to_all | solution.py:209
  18.4 13.4 %all-to-all-done = f32[16,4,16,256]{3,2,1,0:T(8,128)S(1)} async-done(((f32[16,4,16,256]{3,2,1,0:T(8,128)}), f32[16,4,16,256]{3,2,1,0:T(8,128)S(1)}, u32[]{:S(2)}, u32[]{:S(2)}) %all-to-all-start) | async-done | bytes 1048608 | tf_op jit(solution)/shard_map/all_to_all | solution.py:209
  31.8 0.7 collective-permute-start.1
  32.5 1.3 collective-permute-start
  33.8 0.7 collective-permute-start.4
  34.5 0.7 collective-permute-start.3
  35.2 0.7 collective-permute-start.2
  35.8 8.2 %collective-permute-done = f32[3,16,256]{2,1,0:T(8,128)S(1)} collective-permute-done((f32[3,16,256]{2,1,0:T(8,128)S(1)}, f32[3,16,256]{2,1,0:T(8,128)S(1)}, u32[]{:S(2)}, u32[]{:S(2)}) %collective-permute-start) | collective-permute-done | bytes 49184 | tf_op jit(solution)/shard_map/ppermute | solution.py:218
  44.1 1.3 collective-permute-start.6
  45.4 1.3 collective-permute-start.5
  47.4 0.8 collective-permute-done.6
  48.2 1.3 collective-permute-done.5
  49.5 2.1 %broadcast_in_dim.6 = f32[16,3,4,16,256]{4,3,2,1,0:T(8,128)} broadcast(f32[3,4,16,256]{3,2,1,0:T(8,128)S(1)} %slice.50), dimensions={1,2,3,4} | broadcast | bytes 3342336 | tf_op jit(solution)/shard_map/broadcast_in_dim | solution.py:205
  51.7 19.0 %all_to_all.15.mine = f32[16,3,16,256]{3,2,1,0:T(8,128)S(1)} all-to-all(f32[16,3,16,256]{3,2,1,0:T(8,128)S(1)} %broadcast_in_dim.7), channel_id=1, replica_groups=mesh['row_0'=8,'row_1'=2,'col_0'=4,'col_1'=4] {'col_0','col_1'}, dimensions={0} | all-to-all | bytes 1572864 | tf_op jit(solution)/shard_map/all_to_all | solution.py:209
  70.7 0.9 copy-done.1
  71.8 2.3 %collective-permute-done.7.other = f32[16,3,16,256]{3,2,1,0:T(8,128)} collective-permute-done((f32[16,3,16,256]{3,2,1,0:T(8,128)S(1)}, f32[16,3,16,256]{3,2,1,0:T(8,128)}, u32[]{:S(2)}, u32[]{:S(2)}) %collective-permute-start.7) | collective-permute-done | bytes 786464 | tf_op jit(solution)/shard_map/ppermute | solution.py:213
  74.2 7.4 %all-to-all-start.2 = ((f32[16,3,4,16,256]{4,3,2,1,0:T(8,128)}), f32[16,3,4,16,256]{4,3,2,1,0:T(8,128)S(1)}, u32[]{:S(2)}, u32[]{:S(2)}) async-start(f32[16,3,4,16,256]{4,3,2,1,0:T(8,128)} %broadcast_in_dim.6), calls=%async_computation.2 | async-start | bytes 6291456 | tf_op jit(solution)/shard_map/all_to_all | solution.py:209
  81.6 31.2 %corner.1 = (bf16[768,768]{1,0:T(8,128)(2,1)}, bf16[768,768]{1,0:T(8,128)(2,1)}) custom-call(s32[2]{0:T(128)} %pad_add_fusion.place, f32[16,3,16,256]{3,2,1,0:T(8,128)} %copy-done.1, f32[16,3,16,256]{3,2,1,0:T(8,128)} %collective-permute-done.7.other), custom_call_target="tpu_custom_call" | custom-call | tf_op jit(solution)/shard_map/corner/pallas_call | solution.py:112
  112.8 15.9 %all-to-all-done.2.rows = f32[16,3,4,16,256]{4,3,2,1,0:T(8,128)S(1)} async-done(((f32[16,3,4,16,256]{4,3,2,1,0:T(8,128)}), f32[16,3,4,16,256]{4,3,2,1,0:T(8,128)S(1)}, u32[]{:S(2)}, u32[]{:S(2)}) %all-to-all-start.2) | async-done | bytes 3145760 | tf_op jit(solution)/shard_map/all_to_all | solution.py:209
  128.7 1.6 %copy-done = f32[16,3,4,16,256]{4,3,2,1,0:T(8,128)} copy-done((f32[16,3,4,16,256]{4,3,2,1,0:T(8,128)}, f32[16,3,4,16,256]{4,3,2,1,0:T(8,128)S(1)}, u32[]{:S(2)}) %copy-start) | copy-done | bytes 3145752
  130.3 16.1 %panels.1 = f32[1024,1024]{1,0:T(8,128)} custom-call(s32[2]{0:T(128)} %pad_add_fusion.place, f32[4096,1024]{1,0:T(8,128)} %all-gather.2.cloned.1.call-done.lines, bf16[768,768]{1,0:T(8,128)(2,1)} %get-tuple-element.22.inverse_high, bf16[768,768]{1,0:T(8,128)(2,1)} %get-tuple-element.23.inverse_low, f32[16,3,4,16,256]{4,3,2,1,0:T(8,128)} %copy-done, ...), custom_call_target="tpu_custom_call" | custom-call | tf_op jit(solution)/shard_map/panels/pallas_call | solution.py:180
  (21 shorter events, 1.0 us)
Async XLA Ops:
  6.5 122.1 %all-gather.2.cloned.1.call-start = ((), (), s32[]{:S(2)}) async-start(), calls=%async_computation.3 | async-start | bytes 17825792 | tf_op jit(solution)/shard_map/all_gather | solution.py:234
  11.3 20.5 %all-to-all-start = ((f32[16,4,16,256]{3,2,1,0:T(8,128)}), f32[16,4,16,256]{3,2,1,0:T(8,128)S(1)}, u32[]{:S(2)}, u32[]{:S(2)}) async-start(f32[16,4,16,256]{3,2,1,0:T(8,128)} %bitcast.21), calls=%async_computation | async-start | bytes 2097152 | tf_op jit(solution)/shard_map/all_to_all | solution.py:209
  31.8 4.0 %collective-permute-start.1 = (f32[3,16,256]{2,1,0:T(8,128)S(1)}, f32[3,16,256]{2,1,0:T(8,128)S(1)}, u32[]{:S(2)}, u32[]{:S(2)}) collective-permute-start(f32[3,16,256]{2,1,0:T(8,128)S(1)} %fusion), channel_id=1, source_target_pairs={{0,160},{1,161},{2,162},{3,163},{4,164},{5,165},{6,166},{7,167},{8... | collective-permute-start | bytes 147464 | tf_op jit(solution)/shard_map/ppermute | solution.py:219
  32.5 11.6 %collective-permute-start = (f32[3,16,256]{2,1,0:T(8,128)S(1)}, f32[3,16,256]{2,1,0:T(8,128)S(1)}, u32[]{:S(2)}, u32[]{:S(2)}) collective-permute-start(f32[3,16,256]{2,1,0:T(8,128)S(1)} %fusion), channel_id=1, source_target_pairs={{0,96},{1,97},{2,98},{3,99},{4,100},{5,101},{6,102},{7,103},{8,104... | collective-permute-start | bytes 147464 | tf_op jit(solution)/shard_map/ppermute | solution.py:218
  33.8 10.3 %collective-permute-start.4 = (f32[1,16,256]{2,1,0:T(8,128)S(1)}, f32[1,16,256]{2,1,0:T(8,128)S(1)}, u32[]{:S(2)}, u32[]{:S(2)}) collective-permute-start(f32[1,16,256]{2,1,0:T(8,128)S(1)} %slice_bitcast_fusion.3), channel_id=1, source_target_pairs={{32,16},{33,17},{34,18},{35,19},{36,20},{37,21},{38,22},{39,23},{4... | collective-permute-start | bytes 49160 | tf_op jit(solution)/shard_map/ppermute | solution.py:220
  34.5 9.6 %collective-permute-start.3 = (f32[1,16,256]{2,1,0:T(8,128)S(1)}, f32[1,16,256]{2,1,0:T(8,128)S(1)}, u32[]{:S(2)}, u32[]{:S(2)}) collective-permute-start(f32[1,16,256]{2,1,0:T(8,128)S(1)} %slice_bitcast_fusion.3), channel_id=1, source_target_pairs={{32,176},{33,177},{34,178},{35,179},{36,180},{37,181},{38,182},{39... | collective-permute-start | bytes 49160 | tf_op jit(solution)/shard_map/ppermute | solution.py:220
  35.2 9.0 %collective-permute-start.2 = (f32[1,16,256]{2,1,0:T(8,128)S(1)}, f32[1,16,256]{2,1,0:T(8,128)S(1)}, u32[]{:S(2)}, u32[]{:S(2)}) collective-permute-start(f32[1,16,256]{2,1,0:T(8,128)S(1)} %slice_bitcast_fusion.3), channel_id=1, source_target_pairs={{32,112},{33,113},{34,114},{35,115},{36,116},{37,117},{38,118},{39... | collective-permute-start | bytes 49160 | tf_op jit(solution)/shard_map/ppermute | solution.py:220
  44.1 4.1 %collective-permute-start.6 = (f32[3,16,256]{2,1,0:T(8,128)S(1)}, f32[3,16,256]{2,1,0:T(8,128)S(1)}, u32[]{:S(2)}, u32[]{:S(2)}) collective-permute-start(f32[3,16,256]{2,1,0:T(8,128)S(1)} %pad_maximum_fusion), channel_id=1, source_target_pairs={{0,32},{96,64},{160,192},{1,33},{97,65},{161,193},{2,34},{98,66},{... | collective-permute-start | bytes 147464 | tf_op jit(solution)/shard_map/ppermute | solution.py:224
  45.4 4.1 %collective-permute-start.5 = (f32[3,16,256]{2,1,0:T(8,128)S(1)}, f32[3,16,256]{2,1,0:T(8,128)S(1)}, u32[]{:S(2)}, u32[]{:S(2)}) collective-permute-start(f32[3,16,256]{2,1,0:T(8,128)S(1)} %pad_maximum_fusion), channel_id=1, source_target_pairs={{0,224},{96,128},{1,225},{97,129},{2,226},{98,130},{3,227},{99,131... | collective-permute-start | bytes 147464 | tf_op jit(solution)/shard_map/ppermute | solution.py:225
  70.7 0.9 copy-start.1
  71.6 2.6 %collective-permute-start.7 = (f32[16,3,16,256]{3,2,1,0:T(8,128)S(1)}, f32[16,3,16,256]{3,2,1,0:T(8,128)}, u32[]{:S(2)}, u32[]{:S(2)}) collective-permute-start(f32[16,3,16,256]{3,2,1,0:T(8,128)S(1)} %all_to_all.15.mine), channel_id=1, source_target_pairs={{0,16},{16,0},{1,17},{17,1},{2,18},{18,2},{3,19},{19,3},{4,20},{20... | collective-permute-start | bytes 2359304 | tf_op jit(solution)/shard_map/ppermute | solution.py:213
  74.2 54.5 %all-to-all-start.2 = ((f32[16,3,4,16,256]{4,3,2,1,0:T(8,128)}), f32[16,3,4,16,256]{4,3,2,1,0:T(8,128)S(1)}, u32[]{:S(2)}, u32[]{:S(2)}) async-start(f32[16,3,4,16,256]{4,3,2,1,0:T(8,128)} %broadcast_in_dim.6), calls=%async_computation.2 | async-start | bytes 6291456 | tf_op jit(solution)/shard_map/all_to_all | solution.py:209
  128.7 1.6 %copy-start = (f32[16,3,4,16,256]{4,3,2,1,0:T(8,128)}, f32[16,3,4,16,256]{4,3,2,1,0:T(8,128)S(1)}, u32[]{:S(2)}) copy-start(f32[16,3,4,16,256]{4,3,2,1,0:T(8,128)S(1)} %all-to-all-done.2.rows) | copy-start | bytes 9437188
Sparse Core Ops, SparseCore 0:
  9.2 96.2 all-gather.1
